TPU v7x, 32 devices: a whole 2x2x4 slice. The times are simulated.
32 devices in a mesh: fibre: 8 (over z, x), day: 4 (over y, core).
Axes of the slice: x: 2, y: 2, z: 4, core: 2. Of those that a mesh axis runs over, the one named last changes fastest.
Arguments:
- raw_strain: bfloat16 [4, 48, 1024, 512], P('day', None, 'fibre'), may hold values from -6 to 6
- gain_index: int32 [1024], P('fibre'), may hold values from 0 to 7
- dead_mask: int32 [1024], P('fibre'), may hold values 0 or 1
- gain_table: float32 [8], replicated, may hold values from 0.5 to 2
- source_index: int32 [4, 16], replicated, may hold values from 0 to 1023, as said below
Outputs:
- correlations: float32 [64, 1024, 256], P('day', 'fibre')
Inputs may be any that keep to these rules, and one draw needn't show every extreme that they name: `source_index`: the 16 channels of a row are different and all lie in one aligned run of 128 channels, numbers k * 128 .. (k + 1) * 128 - 1. The first row lies in the first run and holds channel 0, the last row lies in the last run and holds the fibre's last channel; the run of each other row is drawn.
All inputs are finite; a program needn't handle non-finite values. No bound on the sum of `dead_mask` on one device may be relied on, other than what follows from the above.
Results may differ from a plain program's by a relative error of at most 0.0019.
Values may be sent and summed in bfloat16 or wider, within the bound.
A program may use at most 128 MiB of HBM per device.

v0:
```python
import math

import jax
import jax.numpy as jnp
from jax import lax
from jax.sharding import PartitionSpec as P

HALF = 16


def with_halo(block, sides, width):
    for axis, dim in sides:
        count = lax.axis_size(axis)
        forward = [(i, i + 1) for i in range(count - 1)]
        backward = [(target, source) for source, target in forward]
        low = lax.ppermute(
            lax.slice_in_dim(block, block.shape[dim] - width, None, axis=dim), axis, forward
        )
        high = lax.ppermute(lax.slice_in_dim(block, 0, width, axis=dim), axis, backward)
        block = jnp.concatenate([low, block, high], axis=dim)
    return block


def entering(part, axis, combine, identity):
    place = lax.axis_index(axis)
    gathered = lax.all_gather(part, axis)
    state = jnp.zeros_like(part) + jnp.asarray(identity, part.dtype)

    def one(step, state):
        return combine(state, lax.dynamic_index_in_dim(gathered, step, 0, False))

    return lax.fori_loop(0, place, one, state)


def dft_table(length, bin_count):
    times = jnp.arange(length, dtype=jnp.int32)
    freqs = jnp.arange(bin_count, dtype=jnp.int32)
    phase = (times[:, None] * freqs[None, :] % length).astype(jnp.float32) * (
        2.0 * math.pi / length
    )
    taper = 0.5 - 0.5 * jnp.cos(times.astype(jnp.float32) * (2.0 * math.pi / length))
    table = jnp.concatenate(
        [taper[:, None] * jnp.cos(phase), -taper[:, None] * jnp.sin(phase)], axis=1
    )
    return table.astype(jnp.bfloat16)


def band_table(bin_count, reach):
    first = jnp.arange(bin_count, dtype=jnp.int32)
    near_bins = (jnp.abs(first[:, None] - first[None, :]) <= reach).astype(jnp.float32)
    counts = jnp.sum(near_bins, axis=0)
    return near_bins / counts[None, :]


def lag_table(length, bin_count, lag_count):
    freqs = jnp.arange(bin_count, dtype=jnp.int32)
    lag_vals = jnp.arange(lag_count, dtype=jnp.int32) - lag_count // 2
    phase = (freqs[:, None] * lag_vals[None, :] % length).astype(jnp.float32) * (
        2.0 * math.pi / length
    )
    weight = jnp.where(freqs == 0, 1.0, 2.0).astype(jnp.float32) / length
    return jnp.concatenate(
        [weight[:, None] * jnp.cos(phase), -weight[:, None] * jnp.sin(phase)], axis=0
    )


def add_terms(earlier, later):
    return earlier + later


def per_device(raw_strain, gain_index, dead_mask, gain_table, source_index):
    seg_count = raw_strain.shape[1]
    chan_count = raw_strain.shape[2]
    length = raw_strain.shape[3]
    bin_count = length // 2
    reach = HALF
    settings = jnp.arange(gain_table.shape[0], dtype=jnp.int32)
    onehot_gain = (gain_index[:, None] == settings[None, :]).astype(jnp.float32)
    channel_gain = jnp.sum(onehot_gain * gain_table[None, :], axis=1) * dead_mask.astype(
        jnp.float32
    )
    calibrated = (raw_strain[0].astype(jnp.float32) * channel_gain[None, :, None]).astype(
        jnp.bfloat16
    )
    padded = with_halo(calibrated, (("fibre", 1),), reach)
    rows_here = jnp.arange(chan_count, dtype=jnp.int32)
    cols_here = jnp.arange(chan_count + 2 * reach, dtype=jnp.int32)
    offset_grid = cols_here[None, :] - rows_here[:, None]
    band_ones = ((offset_grid >= 0) & (offset_grid <= 2 * reach)).astype(jnp.bfloat16)
    window = jnp.einsum("ck,skl->scl", band_ones, padded, preferred_element_type=jnp.float32)
    detrended = calibrated.astype(jnp.float32) - window / (2 * reach + 1)
    local_cum = jnp.cumsum(detrended, axis=1)
    carried = entering(
        local_cum[:, -1, :], "fibre", add_terms, jnp.zeros((seg_count, length), jnp.float32)
    )
    displacement = (local_cum + carried[:, None, :]).astype(jnp.bfloat16)
    spectra = jnp.dot(
        displacement.reshape(-1, length),
        dft_table(length, bin_count),
        preferred_element_type=jnp.float32,
    )
    real_part = spectra[:, :bin_count]
    imag_part = spectra[:, bin_count:]
    power_bins = real_part * real_part + imag_part * imag_part
    smooth = jnp.dot(
        power_bins, band_table(bin_count, bin_count // 4), precision=lax.Precision.HIGHEST
    )
    inv_amp = lax.rsqrt(smooth + 1e-06)
    whitened = (spectra * jnp.concatenate([inv_amp, inv_amp], axis=1)).astype(jnp.bfloat16)
    whitened = whitened.reshape(seg_count, chan_count, length)
    own_index = lax.axis_index("fibre")
    block_count = source_index.shape[0]
    offered = []
    for block in range(block_count):
        holder = source_index[block, 0] // chan_count
        local_rows = jnp.clip(source_index[block] - own_index * chan_count, 0, chan_count - 1)
        offered.append(
            jnp.where(
                holder == own_index,
                jnp.take(whitened, local_rows, axis=1),
                jnp.zeros((), jnp.bfloat16),
            )
        )
    offered_all = jnp.concatenate(offered, axis=1).astype(jnp.float32)
    sources = lax.psum(offered_all.astype(jnp.bfloat16), "fibre")
    chan_re = whitened[:, :, :bin_count]
    chan_im = whitened[:, :, bin_count:]
    inverse = lag_table(length, bin_count, bin_count)
    day_count = lax.axis_size("day")
    src_re = sources[:, :, :bin_count]
    src_im = sources[:, :, bin_count:]
    real_sum = jnp.einsum("gsf,gcf->scf", src_re, chan_re, preferred_element_type=jnp.float32)
    real_sum = real_sum + jnp.einsum(
        "gsf,gcf->scf", src_im, chan_im, preferred_element_type=jnp.float32
    )
    imag_sum = jnp.einsum("gsf,gcf->scf", src_im, chan_re, preferred_element_type=jnp.float32)
    imag_sum = imag_sum - jnp.einsum(
        "gsf,gcf->scf", src_re, chan_im, preferred_element_type=jnp.float32
    )
    stacked = lax.psum_scatter(
        jnp.einsum(
            "scm,mj->scj",
            jnp.concatenate([real_sum, imag_sum], axis=2),
            inverse,
            precision=lax.Precision.HIGHEST,
        ),
        "day",
        scatter_dimension=0,
        tiled=True,
    )
    return stacked * (1.0 / (seg_count * day_count))


def solution(mesh):
    return jax.shard_map(
        per_device,
        mesh=mesh,
        in_specs=(P("day", None, "fibre", None), P("fibre"), P("fibre"), P(), P()),
        out_specs=P("day", "fibre", None),
        check_vma=False,
    )
```

profile of v0, /device:TPU:0, one launch (start us, length us, event | category | flops | bytes accessed | tf_op | source)
XLA Modules:
  0.0 450.3 jit_solution(5346271762334329487)
XLA Ops:
  8.0 5.0 %fusion.3 = bf16[48,128,512]{2,1,0:T(8,128)(2,1)S(1)} fusion(bf16[1,48,128,512]{3,2,1,0:T(8,128)(2,1)} %param.9, f32[128]{0:T(128)S(1)} %convert_multiply_fusion.1), kind=kLoop, calls=%fused_computation.11 | loop fusion | flops 9437184 | bytes 12583424 | tf_op jit(solution)/shard_map/convert_element_type | solution.py:82
  13.0 2.7 copy-done.3
  15.8 4.9 %collective-permute-start = (bf16[48,16,512]{2,1,0:T(8,128)(2,1)S(1)}, bf16[48,16,512]{2,1,0:T(8,128)(2,1)S(1)}, u32[]{:S(2)}, u32[]{:S(2)}) collective-permute-start(bf16[48,16,512]{2,1,0:T(8,128)(2,1)S(1)} %get-tuple-element.48), channel_id=1, source_target_pairs={{0,4},{4,8},{8,12},{12,16},{16,20},{20,24},{24,28},{1,5},{5,9},{9,... | collective-permute-start | bytes 2359304 | tf_op jit(solution)/shard_map/ppermute | solution.py:16
  33.1 3.0 multiply_convert_fusion
  36.1 18.1 %collective-permute-done = bf16[48,16,512]{2,1,0:T(8,128)(2,1)S(1)} collective-permute-done((bf16[48,16,512]{2,1,0:T(8,128)(2,1)S(1)}, bf16[48,16,512]{2,1,0:T(8,128)(2,1)S(1)}, u32[]{:S(2)}, u32[]{:S(2)}) %collective-permute-start) | collective-permute-done | bytes 786464 | tf_op jit(solution)/shard_map/ppermute | solution.py:16
  54.3 8.5 %bitcast_subtract_fusion = f32[48,128,512]{2,1,0:T(8,128)} fusion(bf16[48,128,512]{2,1,0:T(8,128)(2,1)} %copy-done.3, bf16[48,16,512]{2,1,0:T(8,128)(2,1)S(1)} %collective-permute-done.1, bf16[48,16,512]{2,1,0:T(8,128)(2,1)S(1)} %collective-permute-done), kind=kOutput, calls=%fused_computation.12 | convolution fusion | flops 1039745024 | bytes 20447232 | tf_op jit(solution)/shard_map/ck,skl->scl/dot_general | solution.py:90
  62.8 15.4 %fusion.4 = f32[48,128,512]{2,0,1:T(8,128)} fusion(f32[48,128,512]{2,1,0:T(8,128)} %bitcast_subtract_fusion), kind=kOutput, calls=%fused_computation.13 | output fusion | flops 399507456 | bytes 25165824 | tf_op jit(solution)/shard_map/jit(cumsum)/reduce_window_sum | solution.py:92
  79.0 34.4 %all-gather = f32[384,1,512]{2,0,1:T(8,128)S(1)} all-gather(f32[48,1,512]{2,0,1:T(8,128)S(1)} %slice.78), channel_id=2, replica_groups=mesh['fibre'=8,'day'=4] {'fibre'}, dimensions={0}, use_global_device_ids=true | all-gather | bytes 884736 | tf_op jit(solution)/shard_map/all_gather | solution.py:26
  113.7 6.6 %add_convert_fusion = bf16[48,128,512]{2,0,1:T(8,128)(2,1)S(1)} fusion(f32[48,128,512]{2,0,1:T(8,128)} %fusion.4, f32[48,512]{1,0:T(8,128)S(1)} %get-tuple-element.29), kind=kLoop, calls=%fused_computation.15 | loop fusion | flops 6291456 | bytes 18972672 | tf_op jit(solution)/shard_map/convert_element_type | solution.py:96
  120.3 3.6 copy.42
  123.9 4.4 fusion.20
  128.3 5.7 %fusion.6 = f32[6144,256]{1,0:T(8,128)S(1)} fusion(f32[6144,512]{1,0:T(8,128)S(1)} %fusion.20, f32[256]{0:T(256)S(1)} %convert_reduce_fusion), kind=kOutput, calls=%fused_computation.19 | convolution fusion | flops 4838457344 | bytes 18875392 | tf_op jit(solution)/shard_map/dot_general | solution.py:105
  134.0 2.0 fusion.2
  136.1 6.3 %copy.45 = bf16[48,128,512]{2,0,1:T(8,128)(2,1)} copy(bf16[48,128,512]{2,1,0:T(8,128)(2,1)S(1)} %bitcast.55) | data formatting | bytes 12582912 | tf_op jit(solution)/shard_map/reshape | solution.py:110
  142.4 3.4 gather_fusion.3
  145.8 3.4 gather_fusion.2
  149.2 3.4 gather_fusion.1
  152.5 3.4 gather_fusion
  160.6 5.3 %fusion.54 = (bf16[48,128,256]{2,1,0:T(8,128)(2,1)S(1)}, bf16[48,128,256]{2,1,0:T(8,128)(2,1)}) fusion(bf16[48,128,512]{2,1,0:T(8,128)(2,1)} %bitcast.56), kind=kLoop, calls=%fused_computation.103 | loop fusion | bytes 12582912 | tf_op jit(solution)/shard_map/slice | solution.py:127
  165.9 4.9 %copy.57 = bf16[48,128,256]{1,0,2:T(8,128)(2,1)} copy(bf16[48,128,256]{2,1,0:T(8,128)(2,1)} %get-tuple-element.47) | data formatting | bytes 6291456
  170.9 3.4 copy.58
  174.3 112.3 %all-reduce.2.cloned.1.call-done = bf16[48,64,512]{2,0,1:T(8,128)(2,1)} async-done(((bf16[48,64,512]{2,0,1:T(8,128)(2,1)}), bf16[48,64,512]{2,0,1:T(8,128)(2,1)}) %all-reduce.2.cloned.1.call-update) | async-done | bytes 3145744 | tf_op jit(solution)/shard_map/psum | solution.py:125
  286.6 2.1 fusion.56
  288.7 4.8 %copy.49 = bf16[48,64,256]{1,0,2:T(8,128)(2,1)} copy(bf16[48,64,256]{2,0,1:T(8,128)(2,1)S(1)} %get-tuple-element.50) | data formatting | bytes 3145728 | tf_op jit(solution)/shard_map/slice | solution.py:130
  293.5 4.9 %copy.51 = bf16[48,64,256]{1,0,2:T(8,128)(2,1)} copy(bf16[48,64,256]{2,0,1:T(8,128)(2,1)S(1)} %get-tuple-element.51) | data formatting | bytes 3145728 | tf_op jit(solution)/shard_map/slice | solution.py:131
  298.5 4.3 fusion.58
  304.5 7.6 %add_bitcast_fusion = f32[64,128,256]{1,0,2:T(8,128)} fusion(f32[256,128,64]{1,2,0:T(8,128)S(1)} %fusion.58, bf16[48,128,256]{1,0,2:T(8,128)(2,1)} %copy.58, bf16[48,64,256]{1,0,2:T(8,128)(2,1)} %copy.51), kind=kOutput, calls=%fused_computation.17 | convolution fusion | flops 203423744 | bytes 21495808 | tf_op jit(solution)/shard_map/gsf,gcf->scf/dot_general | solution.py:133
  312.1 7.6 %subtract_bitcast_fusion = f32[64,128,256]{1,0,2:T(8,128)} fusion(f32[256,128,64]{1,2,0:T(8,128)S(1)} %fusion.59, bf16[48,128,256]{1,0,2:T(8,128)(2,1)} %copy.58, bf16[48,64,256]{1,0,2:T(8,128)(2,1)} %copy.49), kind=kOutput, calls=%fused_computation.16 | convolution fusion | flops 203423744 | bytes 21495808 | tf_op jit(solution)/shard_map/gsf,gcf->scf/dot_general | solution.py:137
  319.6 7.2 %pad_maximum_fusion = f32[64,128,512]{1,0,2:T(8,128)S(1)} fusion(f32[64,128,256]{1,0,2:T(8,128)} %subtract_bitcast_fusion, f32[64,128,256]{1,0,2:T(8,128)} %add_bitcast_fusion), kind=kLoop, calls=%fused_computation.5 | loop fusion | flops 4194304 | bytes 33554432 | tf_op jit(solution)/shard_map/concatenate | solution.py:143
  326.8 42.3 %fusion = f32[64,128,256]{2,1,0:T(8,128)} fusion(f32[64,128,512]{1,0,2:T(8,128)S(1)} %pad_maximum_fusion, f32[256,256]{1,0:T(8,128)S(1)} %copy-done.4, f32[256,256]{1,0:T(8,128)S(1)} %get-tuple-element.62), kind=kOutput, calls=%fused_computation.6 | convolution fusion | flops 12885032960 | bytes 25690112 | tf_op jit(solution)/shard_map/scm,mj->scj/dot_general | solution.py:141
  369.1 70.8 %reduce-scatter.2.cloned.1.call-done = f32[16,128,256]{2,1,0:T(8,128)} async-done(((f32[64,128,256]{2,1,0:T(8,128)}), f32[16,128,256]{2,1,0:T(8,128)}) %reduce-scatter.2.cloned.1.call-update) | async-done | bytes 2097168 | tf_op jit(solution)/shard_map/reduce_scatter | solution.py:140
  439.9 3.1 broadcast_multiply_fusion
  (39 shorter events, 11.1 us)
Async XLA Ops:
  6.5 280.1 %all-reduce.2.cloned.1.call-start = ((), (), s32[]{:S(2)}) async-start(), calls=%async_computation.1 | async-start | bytes 6291456 | tf_op jit(solution)/shard_map/psum | solution.py:125
  8.0 14.0 %copy-start.5 = (s32[4,16]{1,0:T(4,128)S(1)}, s32[4,16]{1,0:T(4,128)}, u32[]{:S(2)}) copy-start(s32[4,16]{1,0:T(4,128)} %param.13) | copy-start | bytes 772
  13.0 2.7 copy-start.3
  15.8 38.5 %collective-permute-start = (bf16[48,16,512]{2,1,0:T(8,128)(2,1)S(1)}, bf16[48,16,512]{2,1,0:T(8,128)(2,1)S(1)}, u32[]{:S(2)}, u32[]{:S(2)}) collective-permute-start(bf16[48,16,512]{2,1,0:T(8,128)(2,1)S(1)} %get-tuple-element.48), channel_id=1, source_target_pairs={{0,4},{4,8},{8,12},{12,16},{16,20},{20,24},{24,28},{1,5},{5,9},{9,... | collective-permute-start | bytes 2359304 | tf_op jit(solution)/shard_map/ppermute | solution.py:16
  20.7 33.6 %collective-permute-start.1 = (bf16[48,16,512]{2,1,0:T(8,128)(2,1)S(1)}, bf16[48,16,512]{2,1,0:T(8,128)(2,1)S(1)}, u32[]{:S(2)}, u32[]{:S(2)}) collective-permute-start(bf16[48,16,512]{2,1,0:T(8,128)(2,1)S(1)} %get-tuple-element.49), channel_id=1, source_target_pairs={{4,0},{8,4},{12,8},{16,12},{20,16},{24,20},{28,24},{5,1},{9,5},{13... | collective-permute-start | bytes 2359304 | tf_op jit(solution)/shard_map/ppermute | solution.py:19
  136.1 6.3 %copy-start = (bf16[6144,512]{1,0:T(8,128)(2,1)}, bf16[6144,512]{1,0:T(8,128)(2,1)S(1)}, u32[]{:S(2)}) copy-start(bf16[6144,512]{1,0:T(8,128)(2,1)S(1)} %fusion.2) | copy-start | bytes 18874372
  158.6 281.4 %reduce-scatter.2.cloned.1.call-start = ((), (), s32[]{:S(2)}) async-start(), calls=%async_computation.2 | async-start | bytes 10485760 | tf_op jit(solution)/shard_map/reduce_scatter | solution.py:140
  298.4 4.3 copy-start.1
  298.4 4.7 %copy-start.2 = (bf16[48,64,256]{1,0,2:T(8,128)(2,1)S(1)}, bf16[48,64,256]{1,0,2:T(8,128)(2,1)}, u32[]{:S(2)}) copy-start(bf16[48,64,256]{1,0,2:T(8,128)(2,1)} %copy.51) | copy-start | bytes 4718596
  319.6 7.2 %copy-start.4 = (f32[256,256]{1,0:T(8,128)S(1)}, f32[256,256]{1,0:T(8,128)}, u32[]{:S(2)}) copy-start(f32[256,256]{1,0:T(8,128)} %get-tuple-element.63) | copy-start | bytes 786436
Sparse Core Ops, SparseCore 0:
  158.7 127.8 all-reduce.1
  369.2 70.6 reduce-scatter.1
where the time goes:
time: 458 us; the launch traced here: 450 us
  waiting for transfers between devices  201 us (44%)
  matrix products  81.7 us (18%)
  local copies, waits for them, and re-layouts  53.7 us (12%)
  other arithmetic  48.3 us (11%)
  blocking collectives  34.4 us (8%)
  between operations  24.3 us (5%)
  starting transfers between devices  6.4 us (1%)
    psum x1, waiting for transfers between devices, per_device(): sources = lax.psum(offered_all.astype(jnp.bfloat16), 'fibre')  112 us
    reduce_scatter x1, waiting for transfers between devices, per_device(): lax.psum_scatter(jnp.einsum('scm,mj->scj', jnp.concatenate([real_sum, ima...  70.8 us
    dot_general x1, matrix products, per_device(): jnp.einsum('scm,mj->scj', jnp.concatenate([real_sum, imag_sum], axis=2),...  42.3 us
    all_gather x1, blocking collectives, entering(): gathered = lax.all_gather(part, axis)  34.4 us
    ppermute x1, waiting for transfers between devices, with_halo(): lax.ppermute(lax.slice_in_dim(block, block.shape[dim] - width, None, axis...  18.1 us
    another operation x1, other arithmetic, per_device(): local_cum = jnp.cumsum(detrended, axis=1)  15.4 us
    gather x4, local copies, waits for them, and re-layouts, per_device(): jnp.take(whitened, local_rows, axis=1)  13.5 us
    unnamed x14, local copies, waits for them, and re-layouts  11.4 us
  transfers between devices with their start and end apart: 4, of which 3 were waited for; matrix products, arithmetic and copies ran while one was open for 4% of the time, Pallas kernels for 0%

commit v1 on v0

v1 whole, which is shorter than its diff:
```python
import math

import jax
import jax.numpy as jnp
from jax import lax
from jax.sharding import PartitionSpec as P

HALF = 16


def shift_rows(block, axis, width):
    count = lax.axis_size(axis)
    forward = [(i, i + 1) for i in range(count - 1)]
    backward = [(i + 1, i) for i in range(count - 1)]
    low = lax.ppermute(block[:, block.shape[1] - width:], axis, forward)
    high = lax.ppermute(block[:, :width], axis, backward)
    return low, high


def dft_table(length, bin_count):
    times = jnp.arange(length, dtype=jnp.int32)
    freqs = jnp.arange(bin_count, dtype=jnp.int32)
    phase = (times[:, None] * freqs[None, :] % length).astype(jnp.float32) * (
        2.0 * math.pi / length
    )
    taper = 0.5 - 0.5 * jnp.cos(times.astype(jnp.float32) * (2.0 * math.pi / length))
    table = jnp.concatenate(
        [taper[:, None] * jnp.cos(phase), -taper[:, None] * jnp.sin(phase)], axis=1
    )
    return table.astype(jnp.bfloat16)


def band_sum(power, reach):
    bins = power.shape[1]
    first = jnp.arange(bins, dtype=jnp.int32)
    near = jnp.abs(first[:, None] - first[None, :]) <= reach
    counts = jnp.sum(near.astype(jnp.float32), axis=0)
    band = near.astype(jnp.bfloat16)
    high = power.astype(jnp.bfloat16)
    low = (power - high.astype(jnp.float32)).astype(jnp.bfloat16)
    total = jnp.dot(high, band, preferred_element_type=jnp.float32)
    total = total + jnp.dot(low, band, preferred_element_type=jnp.float32)
    return total / counts[None, :]


def lag_table(length, bin_count, lag_count):
    freqs = jnp.arange(bin_count, dtype=jnp.int32)
    lag_vals = jnp.arange(lag_count, dtype=jnp.int32) - lag_count // 2
    phase = (freqs[:, None] * lag_vals[None, :] % length).astype(jnp.float32) * (
        2.0 * math.pi / length
    )
    weight = jnp.where(freqs == 0, 1.0, 2.0).astype(jnp.float32) / length
    return jnp.concatenate(
        [weight[:, None] * jnp.cos(phase), -weight[:, None] * jnp.sin(phase)], axis=0
    )


def whiten(displacement, table):
    segs, rows, length = displacement.shape
    bins = length // 2
    spectra = jnp.dot(
        displacement.reshape(-1, length), table, preferred_element_type=jnp.float32
    )
    real_part = spectra[:, :bins]
    imag_part = spectra[:, bins:]
    smooth = band_sum(real_part * real_part + imag_part * imag_part, bins // 4)
    inv_amp = lax.rsqrt(smooth + 1e-06)
    whitened = (spectra * jnp.concatenate([inv_amp, inv_amp], axis=1)).astype(jnp.bfloat16)
    return whitened.reshape(segs, rows, 2, bins)


def per_device(raw_strain, gain_index, dead_mask, gain_table, source_index):
    seg_count = raw_strain.shape[1]
    chan_count = raw_strain.shape[2]
    length = raw_strain.shape[3]
    bin_count = length // 2
    reach = HALF
    own_index = lax.axis_index("fibre")
    settings = jnp.arange(gain_table.shape[0], dtype=jnp.int32)
    onehot_gain = (gain_index[:, None] == settings[None, :]).astype(jnp.float32)
    channel_gain = jnp.sum(onehot_gain * gain_table[None, :], axis=1) * dead_mask.astype(
        jnp.float32
    )
    calibrated = (raw_strain[0].astype(jnp.float32) * channel_gain[None, :, None]).astype(
        jnp.bfloat16
    )
    low, high = shift_rows(calibrated, "fibre", reach)
    slope = (reach - jnp.arange(reach)).astype(jnp.float32)
    start_part = jnp.sum(calibrated[:, :reach].astype(jnp.float32) * slope[None, :, None], axis=1)
    start_term = lax.psum(jnp.where(own_index == 0, start_part, 0.0), "fibre")
    padded = jnp.concatenate([low, calibrated, high], axis=1)
    rows_here = jnp.arange(chan_count, dtype=jnp.int32)
    cols_here = jnp.arange(chan_count + 2 * reach, dtype=jnp.int32)
    offset = cols_here[None, :] - rows_here[:, None] - reach
    ramp = jnp.where(offset > 0, offset - reach - 1, offset + reach)
    ramp = jnp.where(jnp.abs(offset) <= reach, ramp, 0).astype(jnp.bfloat16)
    local = jnp.einsum("ck,gkt->gct", ramp, padded, preferred_element_type=jnp.float32)
    displacement = ((local + start_term[:, None, :]) * (1.0 / (2 * reach + 1))).astype(
        jnp.bfloat16
    )
    table = dft_table(length, bin_count)

    block_count, block_src = source_index.shape
    source_count = block_count * block_src
    flat = source_index.reshape(-1)
    here = flat // chan_count == own_index
    pick = jnp.where(here, flat - own_index * chan_count, -1)
    choose = (pick[:, None] == rows_here[None, :]).astype(jnp.bfloat16)
    offered = jnp.einsum("sc,gct->gst", choose, displacement, preferred_element_type=jnp.float32)
    chosen = lax.psum(offered.astype(jnp.bfloat16), "fibre")

    whitened = whiten(displacement, table)
    sources = whiten(chosen, table)
    swapped = jnp.stack([sources[:, :, 1], -sources[:, :, 0]], axis=2)

    inverse = lag_table(length, bin_count, bin_count).reshape(2, bin_count, bin_count)
    day = lax.axis_index("day")
    day_count = lax.axis_size("day")
    half_count = day_count // 2
    part = source_count // day_count
    near = [(i, i ^ 1) for i in range(day_count)]
    far = [(i, i ^ 2) for i in range(day_count)]

    def lagged(first):
        one = lax.dynamic_slice_in_dim(sources, first, half_count * part, axis=1)
        two = lax.dynamic_slice_in_dim(swapped, first, half_count * part, axis=1)
        both = jnp.stack([one, two], axis=0)
        cross = jnp.einsum(
            "igspf,gcpf->fisc", both, whitened, preferred_element_type=jnp.float32
        )
        return jnp.einsum("fisc,ifj->scj", cross, inverse, precision=lax.Precision.HIGH)

    def pair_sum(value):
        core = day % 2
        keep = lax.dynamic_slice_in_dim(value, core * part, part, axis=0)
        give = lax.dynamic_slice_in_dim(value, (1 - core) * part, part, axis=0)
        return keep + lax.ppermute(give.astype(jnp.bfloat16), "day", near).astype(jnp.float32)

    upper = day // 2
    other = pair_sum(lagged((1 - upper) * half_count * part))
    came = lax.ppermute(other.astype(jnp.bfloat16), "day", far)
    own = pair_sum(lagged(upper * half_count * part))
    return (own + came.astype(jnp.float32)) * (1.0 / (seg_count * day_count))


def solution(mesh):
    return jax.shard_map(
        per_device,
        mesh=mesh,
        in_specs=(P("day", None, "fibre", None), P("fibre"), P("fibre"), P(), P()),
        out_specs=P("day", "fibre", None),
        check_vma=False,
    )
```

time: 458 us -> 388 us (0.85)
  blocking collectives: 34.4 us -> 0 us
  local copies, waits for them, and re-layouts: 53.7 us -> 83.4 us
  matrix products: 81.7 us -> 52.2 us
  waiting for transfers between devices: 201 us -> 181 us
  between operations: 24.3 us -> 14 us
    reduce_scatter x1 -> x0, waiting for transfers between devices: 70.8 us -> none  [per_device(): lax.psum_scatter(jnp.einsum('scm,mj->scj', jnp.concatenate([real_sum, ima...]
    psum x1 -> x2, waiting for transfers between devices: 112 us -> 157 us  [the longest x1 93.8 us: per_device(): chosen = lax.psum(offered.astype(jnp.bfloat16), 'fibre')]
    all_gather x1 -> x0, blocking collectives: 34.4 us -> none  [entering(): gathered = lax.all_gather(part, axis)]
    dot_general x8 -> x12, matrix products: 81.7 us -> 52.2 us  [the longest x2 18.8 us: lagged(): jnp.einsum('igspf,gcpf->fisc', both, whitened, preferred_element_type=jnp...]
    another operation x0 -> x3, local copies, waits for them, and re-layouts: none -> 28.8 us  [lagged(): both = jnp.stack([one, two], axis=0)]
    dot_general x0 -> x2, local copies, waits for them, and re-layouts: none -> 20 us  [lagged(): jnp.einsum('igspf,gcpf->fisc', both, whitened, preferred_element_type=jnp...]
    reshape x1 -> x4, local copies, waits for them, and re-layouts: 6.31 us -> 25.7 us  [the longest x3 25.6 us: whiten(): return whitened.reshape(segs, rows, 2, bins)]
    slice x7 -> x1, local copies, waits for them, and re-layouts: 18.8 us -> 1.5 us  [shift_rows(): low = lax.ppermute(block[:, block.shape[1] - width:], axis, forward)]
  transfers between devices with their start and end apart: 4 -> 7, of which waited for: 3 -> 4; matrix products, arithmetic and copies ran while one was open for 4% -> 17% of each run, Pallas kernels for 0% -> 0%
where the time goes in v1:
time: 388 us; the launch traced here: 385 us
  waiting for transfers between devices  181 us (47%)
  local copies, waits for them, and re-layouts  83.4 us (21%)
  matrix products  52.2 us (13%)
  other arithmetic  45.4 us (12%)
  between operations  14 us (4%)
  starting transfers between devices  8.92 us (2%)
    psum x1, waiting for transfers between devices, per_device(): chosen = lax.psum(offered.astype(jnp.bfloat16), 'fibre')  93.8 us
    psum x1, waiting for transfers between devices, per_device(): start_term = lax.psum(jnp.where(own_index == 0, start_part, 0.0), 'fibre')  63.2 us
    another operation x3, local copies, waits for them, and re-layouts, lagged(): both = jnp.stack([one, two], axis=0)  28.8 us
    reshape x3, local copies, waits for them, and re-layouts, whiten(): return whitened.reshape(segs, rows, 2, bins)  25.6 us
    ppermute x1, waiting for transfers between devices, per_device(): came = lax.ppermute(other.astype(jnp.bfloat16), 'day', far)  23.2 us
    dot_general x2, local copies, waits for them, and re-layouts, lagged(): jnp.einsum('igspf,gcpf->fisc', both, whitened, preferred_element_type=jnp...  20 us
    another operation x3, other arithmetic, lagged(): both = jnp.stack([one, two], axis=0)  19.2 us
    dot_general x2, matrix products, lagged(): jnp.einsum('igspf,gcpf->fisc', both, whitened, preferred_element_type=jnp...  18.8 us
  transfers between devices with their start and end apart: 7, of which 4 were waited for; matrix products, arithmetic and copies ran while one was open for 17% of the time, Pallas kernels for 0%

profile of v1, /device:TPU:0, one launch (start us, length us, event | category | flops | bytes accessed | tf_op | source)
XLA Modules:
  0.0 384.6 jit_solution(10781733534041413751)
XLA Ops:
  8.0 5.0 %fusion.1 = bf16[48,128,512]{2,1,0:T(8,128)(2,1)S(1)} fusion(bf16[1,48,128,512]{3,2,1,0:T(8,128)(2,1)} %param.5, f32[128]{0:T(128)S(1)} %convert_multiply_fusion.1), kind=kLoop, calls=%fused_computation.3 | loop fusion | flops 9437184 | bytes 12583424 | tf_op jit(solution)/shard_map/convert_element_type | solution.py:84
  13.0 2.6 copy-done.3
  18.3 4.9 %collective-permute-start = (bf16[48,16,512]{2,1,0:T(8,128)(2,1)S(1)}, bf16[48,16,512]{2,1,0:T(8,128)(2,1)S(1)}, u32[]{:S(2)}, u32[]{:S(2)}) collective-permute-start(bf16[48,16,512]{2,1,0:T(8,128)(2,1)S(1)} %get-tuple-element.7), channel_id=1, source_target_pairs={{0,4},{4,8},{8,12},{12,16},{16,20},{20,24},{24,28},{1,5},{5,9},{9,... | collective-permute-start | bytes 2359304 | tf_op jit(solution)/shard_map/ppermute | solution.py:15
  26.4 2.3 multiply_convert_fusion.1
  29.6 63.2 %all-reduce.3.cloned.1.call-done = f32[48,512]{1,0:T(8,128)} async-done(((f32[48,512]{1,0:T(8,128)}), f32[48,512]{1,0:T(8,128)}) %all-reduce.3.cloned.1.call-update) | async-done | bytes 98320 | tf_op jit(solution)/shard_map/psum | solution.py:90
  92.7 4.5 %multiply_convert_fusion = bf16[48,512,128]{1,2,0:T(8,128)(2,1)S(1)} fusion(f32[48,512]{1,0:T(8,128)} %all-reduce.3.cloned.1.call-done, bf16[48,16,512]{2,1,0:T(8,128)(2,1)} %collective-permute-done.1, bf16[48,128,512]{2,1,0:T(8,128)(2,1)} %copy-done.3, bf16[48,16,512]{2,1,0:T(8,128)(2,1)S(1)} %collective-permute-done), kind=kOutput, calls=%fused_computation.4 | convolution fusion | flops 1039847424 | bytes 14254080 | tf_op jit(solution)/shard_map/ck,gkt->gct/dot_general | solution.py:97
  97.3 2.6 copy-done
  99.9 2.8 fusion.25
  102.7 5.5 %fusion.54 = f32[6144,512]{1,0:T(8,128)S(1)} fusion(bf16[6144,512]{1,0:T(8,128)(2,1)} %bitcast.56, bf16[512,256]{1,0:T(8,128)(2,1)S(1)} %get-tuple-element.17, bf16[512,256]{1,0:T(8,128)(2,1)S(1)} %get-tuple-element.18), kind=kOutput, calls=%fused_computation.78 | convolution fusion | flops 3222274048 | bytes 19398656 | tf_op jit(solution)/shard_map/dot_general | solution.py:61
  109.3 1.9 fusion.14
  111.1 4.0 %fusion = bf16[6144,512]{1,0:T(8,128)(2,1)} fusion(f32[6144,512]{1,0:T(8,128)S(1)} %fusion.54, f32[6144,256]{1,0:T(8,128)S(1)} %fusion.14), kind=kLoop, calls=%fused_computation.1 | loop fusion | flops 9437184 | bytes 25165824 | tf_op jit(solution)/shard_map/convert_element_type | solution.py:68
  115.1 9.8 %reshape.99 = bf16[48,128,2,256,1]{3,2,1,0,4:T(2,128)(2,1)} reshape(bf16[6144,512]{1,0:T(8,128)(2,1)} %fusion) | data formatting | bytes 12582912 | tf_op jit(solution)/shard_map/reshape | solution.py:69
  124.9 12.1 %copy.19 = bf16[48,128,2,256,1]{1,0,2,4,3:T(8,128)(2,1)} copy(bf16[48,128,2,256,1]{3,2,1,0,4:T(2,128)(2,1)} %reshape.99) | data formatting | bytes 12582912 | tf_op jit(solution)/shard_map/reshape | solution.py:69
  137.0 93.8 %all-reduce.5.cloned.1.call-done = bf16[3072,512]{1,0:T(8,128)(2,1)} async-done(((bf16[3072,512]{1,0:T(8,128)(2,1)}), bf16[3072,512]{1,0:T(8,128)(2,1)}) %all-reduce.5.cloned.1.call-update) | async-done | bytes 3145744 | tf_op jit(solution)/shard_map/psum | solution.py:110
  230.8 3.7 fusion.55
  236.1 2.5 fusion.16
  238.6 3.8 reshape.92
  242.4 5.8 %fusion.90 = (bf16[48,64,1,256]{3,2,1,0:T(2,128)(2,1)S(1)}, bf16[48,64,1,256]{3,2,1,0:T(2,128)(2,1)S(1)}) fusion(bf16[48,64,2,256]{3,2,1,0:T(2,128)(2,1)S(1)} %reshape.92), kind=kLoop, calls=%fused_computation.133 | loop fusion | flops 786432 | bytes 6291456 | tf_op jit(solution)/shard_map/slice | solution.py:114
  248.1 3.9 %dynamic-slice_bitcast_fusion.1 = (bf16[1,48,32,2,256]{4,3,2,1,0:T(2,128)(2,1)S(1)}, bf16[1,48,32,2,256]{4,3,2,1,0:T(2,128)(2,1)}) fusion(bf16[48,64,2,256]{3,2,1,0:T(2,128)(2,1)S(1)} %reshape.92, s32[]{:T(128)S(6)} %select_n.99, s32[]{:T(128)S(6)} %select_n.105), kind=kLoop, calls=%fused_computation.55 | loop fusion | bytes 6291464 | tf_op jit(solution)/shard_map/stack | solution.py:127
  252.0 8.1 %fusion.39 = (bf16[1,48,32,2,256]{4,3,2,1,0:T(2,128)(2,1)S(1)}, bf16[1,48,32,2,256]{4,3,2,1,0:T(2,128)(2,1)}) fusion(s32[]{:T(128)S(6)} %select_n.99, bf16[48,64,1,256]{3,2,1,0:T(2,128)(2,1)S(1)} %get-tuple-element.12, bf16[48,64,1,256]{3,2,1,0:T(2,128)(2,1)S(1)} %get-tuple-element.11, s32[]{:T(128)S(6)} %select_n.105), kind=kLoop, calls=%fused_computation.57 | loop fusion | flops 6291456 | bytes 6291464 | tf_op jit(solution)/shard_map/stack | solution.py:127
  260.2 4.4 %pad_maximum_fusion = bf16[2,48,32,2,256]{4,3,2,1,0:T(2,128)(2,1)S(1)} fusion(bf16[1,48,32,2,256]{4,3,2,1,0:T(2,128)(2,1)S(1)} %get-tuple-element.5, bf16[1,48,32,2,256]{4,3,2,1,0:T(2,128)(2,1)S(1)} %get-tuple-element.9), kind=kLoop, calls=%fused_computation.35 | loop fusion | flops 1572864 | bytes 6291456 | tf_op jit(solution)/shard_map/stack | solution.py:127
  264.6 12.3 %copy.18 = bf16[2,48,32,2,256]{1,2,3,0,4:T(8,128)(2,1)} copy(bf16[2,48,32,2,256]{4,3,2,1,0:T(2,128)(2,1)S(1)} %pad_maximum_fusion) | data formatting | bytes 6291456 | tf_op jit(solution)/shard_map/stack | solution.py:127
  277.0 6.6 %pad_maximum_fusion.1 = bf16[2,48,32,2,256]{4,3,2,1,0:T(2,128)(2,1)S(1)} fusion(bf16[1,48,32,2,256]{4,3,2,1,0:T(2,128)(2,1)} %get-tuple-element.6, bf16[1,48,32,2,256]{4,3,2,1,0:T(2,128)(2,1)} %get-tuple-element.10), kind=kLoop, calls=%fused_computation.36 | loop fusion | flops 1572864 | bytes 6291456 | tf_op jit(solution)/shard_map/stack | solution.py:127
  283.6 12.5 %copy.22 = bf16[2,48,32,2,256]{1,2,3,0,4:T(8,128)(2,1)} copy(bf16[2,48,32,2,256]{4,3,2,1,0:T(2,128)(2,1)S(1)} %pad_maximum_fusion.1) | data formatting | bytes 6291456 | tf_op jit(solution)/shard_map/stack | solution.py:127
  296.1 10.2 %fusion.92 = f32[256,2,32,128,1]{3,2,4,1,0:T(8,128)} fusion(bf16[2,48,32,2,256]{1,2,3,0,4:T(8,128)(2,1)} %copy.22, bf16[48,128,2,256,1]{1,0,2,4,3:T(8,128)(2,1)} %copy.19), kind=kOutput, calls=%fused_computation.135 | convolution fusion | flops 402653184 | bytes 17825792 | tf_op jit(solution)/shard_map/igspf,gcpf->fisc/dot_general | solution.py:128
  306.3 10.0 %copy.23 = f32[256,2,32,128,1]{0,3,1,2,4:T(8,128)} copy(f32[256,2,32,128,1]{3,2,4,1,0:T(8,128)} %fusion.92) | data formatting | bytes 16777216 | tf_op jit(solution)/shard_map/igspf,gcpf->fisc/dot_general | solution.py:128
  316.3 6.2 %fusion.31 = f32[32,128,256]{2,1,0:T(8,128)S(1)} fusion(f32[2,256,256,1]{2,1,0,3:T(8,128)S(1)} %bitcast.58, f32[256,2,32,128,1]{0,3,1,2,4:T(8,128)} %copy.23), kind=kOutput, calls=%fused_computation.40 | convolution fusion | flops 3221225472 | bytes 13107200 | tf_op jit(solution)/shard_map/fisc,ifj->scj/dot_general | solution.py:131
  322.6 1.9 copy-done.1
  324.8 8.6 %fusion.91 = f32[256,2,32,128,1]{3,2,4,1,0:T(8,128)} fusion(bf16[2,48,32,2,256]{1,2,3,0,4:T(8,128)(2,1)} %copy.18, bf16[48,128,2,256,1]{1,0,2,4,3:T(8,128)(2,1)S(1)} %bitcast.55), kind=kOutput, calls=%fused_computation.134 | convolution fusion | flops 402653184 | bytes 17825792 | tf_op jit(solution)/shard_map/igspf,gcpf->fisc/dot_general | solution.py:128
  333.3 10.0 %copy.20 = f32[256,2,32,128,1]{0,3,1,2,4:T(8,128)} copy(f32[256,2,32,128,1]{3,2,4,1,0:T(8,128)} %fusion.91) | data formatting | bytes 16777216 | tf_op jit(solution)/shard_map/igspf,gcpf->fisc/dot_general | solution.py:128
  343.3 6.2 %fusion.28 = f32[32,128,256]{2,1,0:T(8,128)S(1)} fusion(f32[2,256,256,1]{2,1,0,3:T(8,128)S(1)} %bitcast.59, f32[256,2,32,128,1]{0,3,1,2,4:T(8,128)} %copy.20), kind=kOutput, calls=%fused_computation.39 | convolution fusion | flops 3221225472 | bytes 13107200 | tf_op jit(solution)/shard_map/fisc,ifj->scj/dot_general | solution.py:131
  352.5 23.2 %collective-permute-done.4 = bf16[16,128,256]{2,1,0:T(8,128)(2,1)S(1)} collective-permute-done((bf16[16,128,256]{2,1,0:T(8,128)(2,1)S(1)}, bf16[16,128,256]{2,1,0:T(8,128)(2,1)S(1)}, u32[]{:S(2)}, u32[]{:S(2)}) %collective-permute-start.4) | collective-permute-done | bytes 1048608 | tf_op jit(solution)/shard_map/ppermute | solution.py:141
  (48 shorter events, 15.7 us)
Async XLA Ops:
  6.5 86.2 %all-reduce.3.cloned.1.call-start = ((), (), s32[]{:S(2)}) async-start(), calls=%async_computation | async-start | bytes 196608 | tf_op jit(solution)/shard_map/psum | solution.py:90
  8.0 17.3 %copy-start.5 = (s32[4,16]{1,0:T(4,128)S(1)}, s32[4,16]{1,0:T(4,128)}, u32[]{:S(2)}) copy-start(s32[4,16]{1,0:T(4,128)} %param.9) | copy-start | bytes 772
  13.0 2.7 copy-start.3
  16.7 214.0 %all-reduce.5.cloned.1.call-start = ((), (), s32[]{:S(2)}) async-start(), calls=%async_computation.1 | async-start | bytes 6291456 | tf_op jit(solution)/shard_map/psum | solution.py:110
  18.3 74.4 %collective-permute-start = (bf16[48,16,512]{2,1,0:T(8,128)(2,1)S(1)}, bf16[48,16,512]{2,1,0:T(8,128)(2,1)S(1)}, u32[]{:S(2)}, u32[]{:S(2)}) collective-permute-start(bf16[48,16,512]{2,1,0:T(8,128)(2,1)S(1)} %get-tuple-element.7), channel_id=1, source_target_pairs={{0,4},{4,8},{8,12},{12,16},{16,20},{20,24},{24,28},{1,5},{5,9},{9,... | collective-permute-start | bytes 2359304 | tf_op jit(solution)/shard_map/ppermute | solution.py:15
  23.2 69.5 %collective-permute-start.1 = (bf16[48,16,512]{2,1,0:T(8,128)(2,1)S(1)}, bf16[48,16,512]{2,1,0:T(8,128)(2,1)}, u32[]{:S(2)}, u32[]{:S(2)}) collective-permute-start(bf16[48,16,512]{2,1,0:T(8,128)(2,1)S(1)} %get-tuple-element.8), channel_id=1, source_target_pairs={{4,0},{8,4},{12,8},{16,12},{20,16},{24,20},{28,24},{5,1},{9,5},{13... | collective-permute-start | bytes 2359304 | tf_op jit(solution)/shard_map/ppermute | solution.py:16
  97.3 2.6 copy-start
  306.3 10.0 %copy-start.4 = (f32[512,256]{1,0:T(8,128)S(1)}, f32[512,256]{1,0:T(8,128)}, u32[]{:S(2)}) copy-start(f32[512,256]{1,0:T(8,128)} %pad_maximum_fusion.3) | copy-start | bytes 1572868
  316.3 8.4 %slice-start = ((s8[6291456]{0:T(1024)(128)(4,1)}), s8[4194304]{0:T(1024)(128)(4,1)S(1)}, s32[]{:S(2)}) async-start(s8[6291456]{0:T(1024)(128)(4,1)} %bitcast.54), calls=%async_computation.2 | async-start | bytes 8388608
  316.3 8.4 %slice-start.1 = ((s8[6291456]{0:T(1024)(128)(4,1)}), s8[2097152]{0:T(1024)(128)(4,1)S(1)}, s32[]{:S(2)}) async-start(s8[6291456]{0:T(1024)(128)(4,1)} %bitcast.54), calls=%async_computation.3 | async-start | bytes 4194304
  322.6 1.9 copy-start.1
  324.7 25.5 %collective-permute-start.3 = (bf16[16,128,256]{2,1,0:T(8,128)(2,1)S(1)}, bf16[16,128,256]{2,1,0:T(8,128)(2,1)S(1)}, u32[]{:S(2)}, u32[]{:S(2)}) collective-permute-start(bf16[16,128,256]{2,1,0:T(8,128)(2,1)S(1)} %dynamic-slice_convert_fusion), channel_id=1, source_target_pairs={{0,1},{1,0},{2,3},{3,2},{4,5},{5,4},{6,7},{7,6},{8,9},{9,8},{10,11... | collective-permute-start | bytes 3145736 | tf_op jit(solution)/shard_map/ppermute | solution.py:137
  343.3 6.9 %copy-start.2 = (f32[32,128,256]{2,1,0:T(8,128)S(1)}, f32[32,128,256]{2,1,0:T(8,128)}, u32[]{:S(2)}) copy-start(f32[32,128,256]{2,1,0:T(8,128)} %copy-done.1) | copy-start | bytes 12582916
  349.6 2.8 collective-permute-start.2
  350.5 25.2 %collective-permute-start.4 = (bf16[16,128,256]{2,1,0:T(8,128)(2,1)S(1)}, bf16[16,128,256]{2,1,0:T(8,128)(2,1)S(1)}, u32[]{:S(2)}, u32[]{:S(2)}) collective-permute-start(bf16[16,128,256]{2,1,0:T(8,128)(2,1)S(1)} %add_convert_fusion), channel_id=1, source_target_pairs={{0,2},{1,3},{2,0},{3,1},{4,6},{5,7},{6,4},{7,5},{8,10},{9,11},{10,... | collective-permute-start | bytes 3145736 | tf_op jit(solution)/shard_map/ppermute | solution.py:141
Sparse Core Ops, SparseCore 0:
  16.9 75.8 all-reduce.2
  102.8 127.8 all-reduce.4

commit v2 on v1

--- a/solution.py
+++ b/solution.py
@@ -3,6 +3,8 @@
 import jax
 import jax.numpy as jnp
 from jax import lax
+from jax.experimental import pallas as pl
+from jax.experimental.pallas import tpu as pltpu
 from jax.sharding import PartitionSpec as P
 
 HALF = 16
@@ -66,7 +68,82 @@
     smooth = band_sum(real_part * real_part + imag_part * imag_part, bins // 4)
     inv_amp = lax.rsqrt(smooth + 1e-06)
     whitened = (spectra * jnp.concatenate([inv_amp, inv_amp], axis=1)).astype(jnp.bfloat16)
-    return whitened.reshape(segs, rows, 2, bins)
+    return whitened.reshape(segs, rows, length)
+
+
+def spread(block, axis, root):
+    count = lax.axis_size(axis)
+    step = count // 2
+    while step:
+        pairs = [(i ^ root, (i + step) ^ root) for i in range(0, count, 2 * step)]
+        block = block + lax.ppermute(block, axis, pairs)
+        step //= 2
+    return block
+
+
+def stack_kernel(src_re, src_im, chan_re, chan_im, high_ref, low_ref, out_ref, cross):
+    step = pl.program_id(0)
+    bins, segs, rows = src_re.shape
+    total_bins = high_ref.shape[0] // 2
+    out_rows = rows // 2
+    contract = (((0,), (0,)), ((), ()))
+
+    for place in range(bins):
+        left = jnp.concatenate([src_re[place], src_im[place]], axis=0)
+        right = jnp.concatenate([chan_re[place], chan_im[place]], axis=0)
+        first = pl.multiple_of((step * bins + place) * rows, rows)
+        cross[pl.ds(first, rows), :] = lax.dot_general(
+            left, right, contract, preferred_element_type=jnp.float32
+        )
+
+    @pl.when(step == pl.num_programs(0) - 1)
+    def _():
+        def one(row, carry):
+            total = None
+            for half in range(2):
+                part = cross[pl.ds(half * out_rows + row, total_bins, stride=rows), :]
+                high = part.astype(jnp.bfloat16)
+                low = (part - high.astype(jnp.float32)).astype(jnp.bfloat16)
+                keep = pl.ds(half * total_bins, total_bins)
+                for lhs, rhs in ((high, high_ref), (low, high_ref), (high, low_ref)):
+                    term = lax.dot_general(
+                        lhs, rhs[keep, :], contract, preferred_element_type=jnp.float32
+                    )
+                    total = term if total is None else total + term
+            out_ref[row] = total
+            return carry
+
+        lax.fori_loop(0, out_rows, one, 0)
+
+
+def stack_lags(sources, channels, inverse):
+    length, segs, rows = sources.shape
+    chans = channels.shape[2]
+    lags = inverse.shape[1]
+    step = 32
+    steps = length // 2 // step
+    high = inverse.astype(jnp.bfloat16)
+    low = (inverse - high.astype(jnp.float32)).astype(jnp.bfloat16)
+    whole = pl.BlockSpec((length, lags), lambda i: (0, 0))
+    return pl.pallas_call(
+        stack_kernel,
+        grid=(steps,),
+        in_specs=[
+            pl.BlockSpec((step, segs, rows), lambda i: (i, 0, 0)),
+            pl.BlockSpec((step, segs, rows), lambda i: (i + steps, 0, 0)),
+            pl.BlockSpec((step, segs, chans), lambda i: (i, 0, 0)),
+            pl.BlockSpec((step, segs, chans), lambda i: (i + steps, 0, 0)),
+            whole,
+            whole,
+        ],
+        out_specs=pl.BlockSpec((rows // 2, chans, lags), lambda i: (0, 0, 0)),
+        out_shape=jax.ShapeDtypeStruct((rows // 2, chans, lags), jnp.float32),
+        scratch_shapes=[pltpu.VMEM((length // 2 * rows, chans), jnp.float32)],
+        compiler_params=pltpu.CompilerParams(vmem_limit_bytes=40 << 20),
+        cost_estimate=pl.CostEstimate(
+            flops=20_000_000_000, bytes_accessed=16_000_000, transcendentals=0
+        ),
+    )(sources, sources, channels, channels, high, low)
 
 
 def per_device(raw_strain, gain_index, dead_mask, gain_table, source_index):
@@ -87,7 +164,7 @@
     low, high = shift_rows(calibrated, "fibre", reach)
     slope = (reach - jnp.arange(reach)).astype(jnp.float32)
     start_part = jnp.sum(calibrated[:, :reach].astype(jnp.float32) * slope[None, :, None], axis=1)
-    start_term = lax.psum(jnp.where(own_index == 0, start_part, 0.0), "fibre")
+    start_term = spread(jnp.where(own_index == 0, start_part, 0.0), "fibre", 0)
     padded = jnp.concatenate([low, calibrated, high], axis=1)
     rows_here = jnp.arange(chan_count, dtype=jnp.int32)
     cols_here = jnp.arange(chan_count + 2 * reach, dtype=jnp.int32)
@@ -107,13 +184,30 @@
     pick = jnp.where(here, flat - own_index * chan_count, -1)
     choose = (pick[:, None] == rows_here[None, :]).astype(jnp.bfloat16)
     offered = jnp.einsum("sc,gct->gst", choose, displacement, preferred_element_type=jnp.float32)
-    chosen = lax.psum(offered.astype(jnp.bfloat16), "fibre")
+    offered = offered.astype(jnp.bfloat16)
+    middle = lax.psum(offered[:, block_src:-block_src], "fibre")
+    fibre_count = lax.axis_size("fibre")
+    pieces = []
+    for begin in range(0, seg_count, seg_count // 2):
+        cut = slice(begin, begin + seg_count // 2)
+        first_block = spread(offered[cut, :block_src], "fibre", 0)
+        last_block = spread(offered[cut, -block_src:], "fibre", fibre_count - 1)
+        pieces.append((first_block, last_block))
+    chosen = jnp.concatenate(
+        [
+            jnp.concatenate([piece[0] for piece in pieces], axis=0),
+            middle,
+            jnp.concatenate([piece[1] for piece in pieces], axis=0),
+        ],
+        axis=1,
+    )
 
     whitened = whiten(displacement, table)
     sources = whiten(chosen, table)
-    swapped = jnp.stack([sources[:, :, 1], -sources[:, :, 0]], axis=2)
-
-    inverse = lag_table(length, bin_count, bin_count).reshape(2, bin_count, bin_count)
+    swapped = jnp.concatenate([sources[:, :, bin_count:], -sources[:, :, :bin_count]], axis=2)
+    channels = jnp.transpose(whitened, (2, 0, 1))
+
+    inverse = lag_table(length, bin_count, bin_count)
     day = lax.axis_index("day")
     day_count = lax.axis_size("day")
     half_count = day_count // 2
@@ -124,11 +218,8 @@
     def lagged(first):
         one = lax.dynamic_slice_in_dim(sources, first, half_count * part, axis=1)
         two = lax.dynamic_slice_in_dim(swapped, first, half_count * part, axis=1)
-        both = jnp.stack([one, two], axis=0)
-        cross = jnp.einsum(
-            "igspf,gcpf->fisc", both, whitened, preferred_element_type=jnp.float32
-        )
-        return jnp.einsum("fisc,ifj->scj", cross, inverse, precision=lax.Precision.HIGH)
+        both = jnp.transpose(jnp.concatenate([one, two], axis=1), (2, 0, 1))
+        return stack_lags(both, channels, inverse)
 
     def pair_sum(value):
         core = day % 2

time: 388 us -> 336 us (0.87)
  waiting for transfers between devices: 181 us -> 110 us
  Pallas kernels: 0 us -> 48.1 us
  local copies, waits for them, and re-layouts: 83.4 us -> 44.1 us
  matrix products: 52.2 us -> 21 us
  starting transfers between devices: 8.92 us -> 35.1 us
  other arithmetic: 45.4 us -> 62.3 us
    psum x2 -> x1, waiting for transfers between devices: 157 us -> 28.3 us  [per_device(): middle = lax.psum(offered[:, block_src:-block_src], 'fibre')]
    ppermute x0 -> x15, waiting for transfers between devices: none -> 58.3 us  [spread(): block = block + lax.ppermute(block, axis, pairs)]
    pallas_call x0 -> x2, Pallas kernels: none -> 48.1 us  [stack_lags(): pl.pallas_call(stack_kernel, grid=(steps,), in_specs=[pl.BlockSpec((step,...]
    dot_general x4 -> x0, matrix products: 31.2 us -> none  [the longest x2 18.8 us: lagged(): jnp.einsum('igspf,gcpf->fisc', both, whitened, preferred_element_type=jnp...]
    ppermute x0 -> x15, starting transfers between devices: none -> 29.5 us  [spread(): block = block + lax.ppermute(block, axis, pairs)]
    another operation x3 -> x0, local copies, waits for them, and re-layouts: 28.8 us -> none  [lagged(): both = jnp.stack([one, two], axis=0)]
    dot_general x2 -> x0, local copies, waits for them, and re-layouts: 20 us -> none  [lagged(): jnp.einsum('igspf,gcpf->fisc', both, whitened, preferred_element_type=jnp...]
    unnamed x16 -> x22, local copies, waits for them, and re-layouts: 7.23 us -> 27 us
  transfers between devices with their start and end apart: 7 -> 21, of which waited for: 4 -> 9; matrix products, arithmetic and copies ran while one was open for 17% -> 13% of each run, Pallas kernels for 0% -> 7%
where the time goes in v2:
time: 336 us; the launch traced here: 335 us
  waiting for transfers between devices  110 us (33%)
  other arithmetic  62.3 us (19%)
  Pallas kernels  48.1 us (14%)
  local copies, waits for them, and re-layouts  44.1 us (13%)
  starting transfers between devices  35.1 us (10%)
  matrix products  21 us (6%)
  between operations  13.9 us (4%)
    ppermute x15, waiting for transfers between devices, spread(): block = block + lax.ppermute(block, axis, pairs)  58.3 us
    pallas_call x2, Pallas kernels, stack_lags(): pl.pallas_call(stack_kernel, grid=(steps,), in_specs=[pl.BlockSpec((step,...  48.1 us
    ppermute x15, starting transfers between devices, spread(): block = block + lax.ppermute(block, axis, pairs)  29.5 us
    psum x1, waiting for transfers between devices, per_device(): middle = lax.psum(offered[:, block_src:-block_src], 'fibre')  28.3 us
    unnamed x22, local copies, waits for them, and re-layouts  27 us
    ppermute x1, waiting for transfers between devices, per_device(): came = lax.ppermute(other.astype(jnp.bfloat16), 'day', far)  23.2 us
    concatenate x1, other arithmetic, per_device(): jnp.concatenate([sources[:, :, bin_count:], -sources[:, :, :bin_count]],...  13.8 us
    convert_element_type x2, other arithmetic, whiten(): (spectra * jnp.concatenate([inv_amp, inv_amp], axis=1)).astype(jnp.bfloat16)  13.5 us
  transfers between devices with their start and end apart: 21, of which 9 were waited for; matrix products, arithmetic and copies ran while one was open for 13% of the time, Pallas kernels for 7%

profile of v2, /device:TPU:0, one launch (start us, length us, event | category | flops | bytes accessed | tf_op | source)
XLA Modules:
  0.0 334.8 jit_solution(1799527177443768830)
XLA Ops:
  8.0 5.0 %fusion.1 = bf16[48,128,512]{2,1,0:T(8,128)(2,1)S(1)} fusion(bf16[1,48,128,512]{3,2,1,0:T(8,128)(2,1)} %param.5, f32[128]{0:T(128)S(1)} %convert_multiply_fusion.1), kind=kLoop, calls=%fused_computation.3 | loop fusion | flops 9437184 | bytes 12583424 | tf_op jit(solution)/shard_map/convert_element_type | solution.py:161
  13.4 5.9 %collective-permute-start.2 = (f32[48,512]{1,0:T(8,128)S(1)}, f32[48,512]{1,0:T(8,128)S(1)}, u32[]{:S(2)}, u32[]{:S(2)}) collective-permute-start(f32[48,512]{1,0:T(8,128)S(1)} %broadcast_select_fusion), channel_id=1, source_target_pairs={{0,16},{1,17},{2,18},{3,19}} | collective-permute-start | bytes 294920 | tf_op jit(solution)/shard_map/ppermute | solution.py:79
  19.6 2.2 collective-permute-start
  23.1 2.3 multiply_convert_fusion.1
  26.8 4.4 %collective-permute-start.3 = (f32[48,512]{1,0:T(8,128)S(1)}, f32[48,512]{1,0:T(8,128)S(1)}, u32[]{:S(2)}, u32[]{:S(2)}) collective-permute-start(f32[48,512]{1,0:T(8,128)S(1)} %fusion.82), channel_id=1, source_target_pairs={{0,8},{16,24},{1,9},{17,25},{2,10},{18,26},{3,11},{19,27}} | collective-permute-start | bytes 294920 | tf_op jit(solution)/shard_map/ppermute | solution.py:79
  31.2 2.2 collective-permute-done.3
  34.8 21.8 %collective-permute-done.4 = f32[48,512]{1,0:T(8,128)S(1)} collective-permute-done((f32[48,512]{1,0:T(8,128)S(1)}, f32[48,512]{1,0:T(8,128)S(1)}, u32[]{:S(2)}, u32[]{:S(2)}) %collective-permute-start.4) | collective-permute-done | bytes 98336 | tf_op jit(solution)/shard_map/ppermute | solution.py:79
  56.6 4.5 %multiply_convert_fusion = bf16[48,512,128]{1,2,0:T(8,128)(2,1)S(1)} fusion(f32[48,512]{1,0:T(8,128)S(1)} %add.149, bf16[48,16,512]{2,1,0:T(8,128)(2,1)} %collective-permute-done.1, bf16[48,128,512]{2,1,0:T(8,128)(2,1)} %copy-done.5, bf16[48,16,512]{2,1,0:T(8,128)(2,1)} %collective-permute-done), kind=kOutput, calls=%fused_computation.4 | convolution fusion | flops 1039847424 | bytes 14254080 | tf_op jit(solution)/shard_map/ck,gkt->gct/dot_general | solution.py:174
  67.5 4.3 %collective-permute-start.5 = (bf16[24,16,512]{2,1,0:T(8,128)(2,1)S(1)}, bf16[24,16,512]{2,1,0:T(8,128)(2,1)S(1)}, u32[]{:S(2)}, u32[]{:S(2)}) collective-permute-start(bf16[24,16,512]{2,1,0:T(8,128)(2,1)S(1)} %get-tuple-element.17), channel_id=1, source_target_pairs={{0,16},{1,17},{2,18},{3,19}} | collective-permute-start | bytes 1179656 | tf_op jit(solution)/shard_map/ppermute | solution.py:79
  73.9 5.5 %fusion.42 = f32[6144,512]{1,0:T(8,128)S(1)} fusion(bf16[6144,512]{1,0:T(8,128)(2,1)} %bitcast.28, bf16[512,256]{1,0:T(8,128)(2,1)S(1)} %get-tuple-element.25, bf16[512,256]{1,0:T(8,128)(2,1)S(1)} %get-tuple-element.26), kind=kOutput, calls=%fused_computation.70 | convolution fusion | flops 3222274048 | bytes 19398656 | tf_op jit(solution)/shard_map/dot_general | solution.py:63
  80.5 2.7 collective-permute-done.5
  83.2 15.8 %collective-permute-done.8 = bf16[24,16,512]{2,1,0:T(8,128)(2,1)} collective-permute-done((bf16[24,16,512]{2,1,0:T(8,128)(2,1)S(1)}, bf16[24,16,512]{2,1,0:T(8,128)(2,1)}, u32[]{:S(2)}, u32[]{:S(2)}) %collective-permute-start.8) | collective-permute-done | bytes 393248 | tf_op jit(solution)/shard_map/ppermute | solution.py:79
  104.4 3.7 %fusion.10 = f32[6144,256]{1,0:T(8,128)} fusion(f32[6144,256]{1,0:T(8,128)S(1)} %fusion.26, f32[256]{0:T(256)S(1)} %convert_reduce_fusion, f32[6144,512]{1,0:T(8,128)S(1)} %fusion.42), kind=kOutput, calls=%fused_computation.18 | convolution fusion | flops 821231616 | bytes 25166848 | tf_op jit(solution)/shard_map/dot_general | solution.py:44
  108.1 7.1 %collective-permute-done.6 = bf16[24,16,512]{2,1,0:T(8,128)(2,1)S(1)} collective-permute-done((bf16[24,16,512]{2,1,0:T(8,128)(2,1)S(1)}, bf16[24,16,512]{2,1,0:T(8,128)(2,1)S(1)}, u32[]{:S(2)}, u32[]{:S(2)}) %collective-permute-start.6) | collective-permute-done | bytes 393248 | tf_op jit(solution)/shard_map/ppermute | solution.py:79
  116.7 8.7 %collective-permute-done.9 = bf16[24,16,512]{2,1,0:T(8,128)(2,1)S(1)} collective-permute-done((bf16[24,16,512]{2,1,0:T(8,128)(2,1)S(1)}, bf16[24,16,512]{2,1,0:T(8,128)(2,1)S(1)}, u32[]{:S(2)}, u32[]{:S(2)}) %collective-permute-start.9) | collective-permute-done | bytes 393248 | tf_op jit(solution)/shard_map/ppermute | solution.py:79
  130.4 9.6 %fusion = bf16[6144,512]{1,0:T(8,128)(2,1)} fusion(f32[6144,512]{1,0:T(8,128)S(1)} %fusion.42, f32[6144,256]{1,0:T(8,128)} %fusion.10), kind=kLoop, calls=%fused_computation.1 | loop fusion | flops 9437184 | bytes 25165824 | tf_op jit(solution)/shard_map/convert_element_type | solution.py:70
  140.0 9.1 %copy.34 = bf16[48,128,512]{1,0,2:T(8,128)(2,1)} copy(bf16[48,128,512]{2,1,0:T(8,128)(2,1)} %bitcast.31) | data formatting | bytes 12582912 | tf_op jit(solution)/shard_map/reshape | solution.py:71
  152.6 28.3 %all-reduce.2.cloned.1.call-done = bf16[48,32,512]{2,1,0:T(8,128)(2,1)} async-done(((bf16[48,32,512]{2,1,0:T(8,128)(2,1)}), bf16[48,32,512]{2,1,0:T(8,128)(2,1)}) %all-reduce.2.cloned.1.call-update) | async-done | bytes 1572880 | tf_op jit(solution)/shard_map/psum | solution.py:188
  185.0 2.7 fusion.21
  187.6 3.8 %fusion.14 = bf16[3072,512]{1,0:T(8,128)(2,1)S(1)} fusion(f32[3072,512]{1,0:T(8,128)S(1)} %fusion.43, f32[3072,256]{1,0:T(8,128)} %fusion.21), kind=kLoop, calls=%fused_computation.25 | loop fusion | flops 4718592 | bytes 12582912 | tf_op jit(solution)/shard_map/convert_element_type | solution.py:70
  194.7 5.3 %copy.37 = bf16[48,64,256]{1,0,2:T(8,128)(2,1)} copy(bf16[48,64,256]{2,1,0:T(8,128)(2,1)} %get-tuple-element.11) | data formatting | bytes 3145728
  200.0 4.2 %neg.20 = bf16[48,64,256]{1,0,2:T(8,128)(2,1)} negate(bf16[48,64,256]{1,0,2:T(8,128)(2,1)} %copy.37) | non-fusion elementwise | flops 786432 | bytes 3145728 | tf_op jit(solution)/shard_map/neg | solution.py:207
  204.2 3.9 %copy.36 = bf16[48,64,256]{1,0,2:T(8,128)(2,1)} copy(bf16[48,64,256]{2,1,0:T(8,128)(2,1)S(1)} %get-tuple-element.12) | data formatting | bytes 3145728
  208.1 3.4 %constant_dynamic-slice_fusion.1 = (bf16[48,32,512]{2,1,0:T(8,128)(2,1)}, bf16[48,32,512]{2,1,0:T(8,128)(2,1)S(1)}) fusion(bf16[48,64,512]{2,1,0:T(8,128)(2,1)} %bitcast.30, s32[]{:T(128)S(6)} %select_n.99, s32[]{:T(128)S(6)} %select_n.105), kind=kLoop, calls=%fused_computation.101 | loop fusion | bytes 6291464 | tf_op jit(solution)/shard_map/dynamic_slice | solution.py:219
  211.5 8.0 %copy.35 = bf16[48,32,512]{1,0,2:T(8,128)(2,1)} copy(bf16[48,32,512]{2,1,0:T(8,128)(2,1)} %get-tuple-element.9) | data formatting | bytes 3145728
  219.5 6.9 %copy.38 = bf16[48,32,512]{1,0,2:T(8,128)(2,1)} copy(bf16[48,32,512]{2,1,0:T(8,128)(2,1)S(1)} %get-tuple-element.10) | data formatting | bytes 3145728
  226.4 13.8 %fusion.12 = (bf16[48,32,512]{1,0,2:T(8,128)(2,1)}, bf16[48,32,512]{1,0,2:T(8,128)(2,1)}) fusion(s32[]{:T(128)S(6)} %select_n.99, bf16[48,64,256]{1,0,2:T(8,128)(2,1)} %copy.36, bf16[48,64,256]{1,0,2:T(8,128)(2,1)} %neg.20, s32[]{:T(128)S(6)} %select_n.105), kind=kLoop, calls=%fused_computation.20 | loop fusion | flops 6291456 | bytes 6291464 | tf_op jit(solution)/shard_map/concatenate | solution.py:207
  240.2 5.7 %maximum_bitcast_fusion.1.src_re.src_im = bf16[512,48,64]{2,1,0:T(8,128)(2,1)S(1)} fusion(bf16[48,32,512]{1,0,2:T(8,128)(2,1)} %get-tuple-element.6, bf16[48,32,512]{1,0,2:T(8,128)(2,1)S(1)} %copy-done.2), kind=kLoop, calls=%fused_computation.27 | loop fusion | flops 6291456 | bytes 6291456 | tf_op jit(solution)/shard_map/transpose | solution.py:221
  246.0 24.1 %shard_map.56 = f32[32,128,256]{2,1,0:T(8,128)S(1)} custom-call(bf16[512,48,64]{2,1,0:T(8,128)(2,1)S(1)} %maximum_bitcast_fusion.1.src_re.src_im, bf16[512,48,64]{2,1,0:T(8,128)(2,1)S(1)} %maximum_bitcast_fusion.1.src_re.src_im, bf16[512,48,128]{2,1,0:T(8,128)(2,1)} %bitcast.35, bf16[512,48,128]{2,1,0:T(8,128)(2,1)} %bitcast.36, ...), custom_call_target="tpu_custom_call" | custom-call | flops 20000000000 | bytes 16000000 | tf_op jit(solution)/shard_map/pallas_call | solution.py:128
  270.4 5.6 %maximum_bitcast_fusion.src_re.src_im = bf16[512,48,64]{2,1,0:T(8,128)(2,1)S(1)} fusion(bf16[48,32,512]{1,0,2:T(8,128)(2,1)} %get-tuple-element.5, bf16[48,32,512]{1,0,2:T(8,128)(2,1)S(1)} %bitcast.33), kind=kLoop, calls=%fused_computation.26 | loop fusion | flops 6291456 | bytes 6291456 | tf_op jit(solution)/shard_map/transpose | solution.py:221
  276.0 24.0 %shard_map.55 = f32[32,128,256]{2,1,0:T(8,128)S(1)} custom-call(bf16[512,48,64]{2,1,0:T(8,128)(2,1)S(1)} %maximum_bitcast_fusion.src_re.src_im, bf16[512,48,64]{2,1,0:T(8,128)(2,1)S(1)} %maximum_bitcast_fusion.src_re.src_im, bf16[512,48,128]{2,1,0:T(8,128)(2,1)} %bitcast.37, bf16[512,48,128]{2,1,0:T(8,128)(2,1)} %bitcast.38, ...), custom_call_target="tpu_custom_call" | custom-call | flops 20000000000 | bytes 16000000 | tf_op jit(solution)/shard_map/pallas_call | solution.py:128
  302.9 23.2 %collective-permute-done.19 = bf16[16,128,256]{2,1,0:T(8,128)(2,1)S(1)} collective-permute-done((bf16[16,128,256]{2,1,0:T(8,128)(2,1)S(1)}, bf16[16,128,256]{2,1,0:T(8,128)(2,1)S(1)}, u32[]{:S(2)}, u32[]{:S(2)}) %collective-permute-start.19) | collective-permute-done | bytes 1048608 | tf_op jit(solution)/shard_map/ppermute | solution.py:232
  (90 shorter events, 43.1 us)
Async XLA Ops:
  6.5 174.4 %all-reduce.2.cloned.1.call-start = ((), (), s32[]{:S(2)}) async-start(), calls=%async_computation | async-start | bytes 3145728 | tf_op jit(solution)/shard_map/psum | solution.py:188
  8.0 18.6 %copy-start.6 = (s32[4,16]{1,0:T(4,128)S(1)}, s32[4,16]{1,0:T(4,128)}, u32[]{:S(2)}) copy-start(s32[4,16]{1,0:T(4,128)} %param.9) | copy-start | bytes 772
  13.0 6.4 %copy-start.5 = (bf16[48,128,512]{2,1,0:T(8,128)(2,1)}, bf16[48,128,512]{2,1,0:T(8,128)(2,1)S(1)}, u32[]{:S(2)}) copy-start(bf16[48,128,512]{2,1,0:T(8,128)(2,1)S(1)} %fusion.1) | copy-start | bytes 18874372
  13.4 13.3 %collective-permute-start.2 = (f32[48,512]{1,0:T(8,128)S(1)}, f32[48,512]{1,0:T(8,128)S(1)}, u32[]{:S(2)}, u32[]{:S(2)}) collective-permute-start(f32[48,512]{1,0:T(8,128)S(1)} %broadcast_select_fusion), channel_id=1, source_target_pairs={{0,16},{1,17},{2,18},{3,19}} | collective-permute-start | bytes 294920 | tf_op jit(solution)/shard_map/ppermute | solution.py:79
  19.6 37.1 %collective-permute-start = (bf16[48,16,512]{2,1,0:T(8,128)(2,1)S(1)}, bf16[48,16,512]{2,1,0:T(8,128)(2,1)}, u32[]{:S(2)}, u32[]{:S(2)}) collective-permute-start(bf16[48,16,512]{2,1,0:T(8,128)(2,1)S(1)} %get-tuple-element.7), channel_id=1, source_target_pairs={{0,4},{4,8},{8,12},{12,16},{16,20},{20,24},{24,28},{1,5},{5,9},{9,... | collective-permute-start | bytes 2359304 | tf_op jit(solution)/shard_map/ppermute | solution.py:17
  21.7 34.9 %collective-permute-start.1 = (bf16[48,16,512]{2,1,0:T(8,128)(2,1)S(1)}, bf16[48,16,512]{2,1,0:T(8,128)(2,1)}, u32[]{:S(2)}, u32[]{:S(2)}) collective-permute-start(bf16[48,16,512]{2,1,0:T(8,128)(2,1)S(1)} %get-tuple-element.8), channel_id=1, source_target_pairs={{4,0},{8,4},{12,8},{16,12},{20,16},{24,20},{28,24},{5,1},{9,5},{13... | collective-permute-start | bytes 2359304 | tf_op jit(solution)/shard_map/ppermute | solution.py:18
  26.8 6.6 %collective-permute-start.3 = (f32[48,512]{1,0:T(8,128)S(1)}, f32[48,512]{1,0:T(8,128)S(1)}, u32[]{:S(2)}, u32[]{:S(2)}) collective-permute-start(f32[48,512]{1,0:T(8,128)S(1)} %fusion.82), channel_id=1, source_target_pairs={{0,8},{16,24},{1,9},{17,25},{2,10},{18,26},{3,11},{19,27}} | collective-permute-start | bytes 294920 | tf_op jit(solution)/shard_map/ppermute | solution.py:79
  33.4 23.2 %collective-permute-start.4 = (f32[48,512]{1,0:T(8,128)S(1)}, f32[48,512]{1,0:T(8,128)S(1)}, u32[]{:S(2)}, u32[]{:S(2)}) collective-permute-start(f32[48,512]{1,0:T(8,128)S(1)} %add.148), channel_id=1, source_target_pairs={{0,4},{8,12},{16,20},{24,28},{1,5},{9,13},{17,21},{25,29},{2,6},{1... | collective-permute-start | bytes 294920 | tf_op jit(solution)/shard_map/ppermute | solution.py:79
  61.2 2.8 copy-start
  62.4 2.6 copy-start.3
  66.2 14.3 %collective-permute-start.11 = (bf16[24,16,512]{2,1,0:T(8,128)(2,1)}, bf16[24,16,512]{2,1,0:T(8,128)(2,1)S(1)}, u32[]{:S(2)}, u32[]{:S(2)}) collective-permute-start(bf16[24,16,512]{2,1,0:T(8,128)(2,1)} %get-tuple-element.19), channel_id=1, source_target_pairs={{28,12},{29,13},{30,14},{31,15}} | collective-permute-start | bytes 1179656 | tf_op jit(solution)/shard_map/ppermute | solution.py:79
  66.8 13.6 %collective-permute-start.14 = (bf16[24,16,512]{2,1,0:T(8,128)(2,1)S(1)}, bf16[24,16,512]{2,1,0:T(8,128)(2,1)S(1)}, u32[]{:S(2)}, u32[]{:S(2)}) collective-permute-start(bf16[24,16,512]{2,1,0:T(8,128)(2,1)S(1)} %get-tuple-element.18), channel_id=1, source_target_pairs={{28,12},{29,13},{30,14},{31,15}} | collective-permute-start | bytes 1179656 | tf_op jit(solution)/shard_map/ppermute | solution.py:79
  67.5 15.6 %collective-permute-start.5 = (bf16[24,16,512]{2,1,0:T(8,128)(2,1)S(1)}, bf16[24,16,512]{2,1,0:T(8,128)(2,1)S(1)}, u32[]{:S(2)}, u32[]{:S(2)}) collective-permute-start(bf16[24,16,512]{2,1,0:T(8,128)(2,1)S(1)} %get-tuple-element.17), channel_id=1, source_target_pairs={{0,16},{1,17},{2,18},{3,19}} | collective-permute-start | bytes 1179656 | tf_op jit(solution)/shard_map/ppermute | solution.py:79
  71.8 27.1 %collective-permute-start.8 = (bf16[24,16,512]{2,1,0:T(8,128)(2,1)S(1)}, bf16[24,16,512]{2,1,0:T(8,128)(2,1)}, u32[]{:S(2)}, u32[]{:S(2)}) collective-permute-start(bf16[24,16,512]{2,1,0:T(8,128)(2,1)S(1)} %get-tuple-element.20), channel_id=1, source_target_pairs={{0,16},{1,17},{2,18},{3,19}} | collective-permute-start | bytes 1179656 | tf_op jit(solution)/shard_map/ppermute | solution.py:79
  79.4 19.5 %copy-start.4 = (bf16[48,64,512]{2,1,0:T(8,128)(2,1)S(1)}, bf16[48,64,512]{2,1,0:T(8,128)(2,1)}, u32[]{:S(2)}) copy-start(bf16[48,64,512]{2,1,0:T(8,128)(2,1)} %copy-done.3) | copy-start | bytes 9437188
  100.2 15.0 %collective-permute-start.6 = (bf16[24,16,512]{2,1,0:T(8,128)(2,1)S(1)}, bf16[24,16,512]{2,1,0:T(8,128)(2,1)S(1)}, u32[]{:S(2)}, u32[]{:S(2)}) collective-permute-start(bf16[24,16,512]{2,1,0:T(8,128)(2,1)S(1)} %get-tuple-element.13), channel_id=1, source_target_pairs={{0,8},{16,24},{1,9},{17,25},{2,10},{18,26},{3,11},{19,27}} | collective-permute-start | bytes 1179656 | tf_op jit(solution)/shard_map/ppermute | solution.py:79
  101.5 23.8 %collective-permute-start.9 = (bf16[24,16,512]{2,1,0:T(8,128)(2,1)S(1)}, bf16[24,16,512]{2,1,0:T(8,128)(2,1)S(1)}, u32[]{:S(2)}, u32[]{:S(2)}) collective-permute-start(bf16[24,16,512]{2,1,0:T(8,128)(2,1)S(1)} %get-tuple-element.14), channel_id=1, source_target_pairs={{0,8},{16,24},{1,9},{17,25},{2,10},{18,26},{3,11},{19,27}} | collective-permute-start | bytes 1179656 | tf_op jit(solution)/shard_map/ppermute | solution.py:79
  102.8 24.7 %collective-permute-start.12 = (bf16[24,16,512]{2,1,0:T(8,128)(2,1)S(1)}, bf16[24,16,512]{2,1,0:T(8,128)(2,1)S(1)}, u32[]{:S(2)}, u32[]{:S(2)}) collective-permute-start(bf16[24,16,512]{2,1,0:T(8,128)(2,1)S(1)} %get-tuple-element.15), channel_id=1, source_target_pairs={{28,20},{12,4},{29,21},{13,5},{30,22},{14,6},{31,23},{15,7}} | collective-permute-start | bytes 1179656 | tf_op jit(solution)/shard_map/ppermute | solution.py:79
  103.5 25.4 %collective-permute-start.15 = (bf16[24,16,512]{2,1,0:T(8,128)(2,1)S(1)}, bf16[24,16,512]{2,1,0:T(8,128)(2,1)S(1)}, u32[]{:S(2)}, u32[]{:S(2)}) collective-permute-start(bf16[24,16,512]{2,1,0:T(8,128)(2,1)S(1)} %get-tuple-element.16), channel_id=1, source_target_pairs={{28,20},{12,4},{29,21},{13,5},{30,22},{14,6},{31,23},{15,7}} | collective-permute-start | bytes 1179656 | tf_op jit(solution)/shard_map/ppermute | solution.py:79
  115.3 33.8 %collective-permute-start.7 = (bf16[24,16,512]{2,1,0:T(8,128)(2,1)S(1)}, bf16[24,16,512]{2,1,0:T(8,128)(2,1)S(1)}, u32[]{:S(2)}, u32[]{:S(2)}) collective-permute-start(bf16[24,16,512]{2,1,0:T(8,128)(2,1)S(1)} %add.153), channel_id=1, source_target_pairs={{0,4},{8,12},{16,20},{24,28},{1,5},{9,13},{17,21},{25,29},{2,6},{1... | collective-permute-start | bytes 1179656 | tf_op jit(solution)/shard_map/ppermute | solution.py:79
  125.5 23.8 %collective-permute-start.10 = (bf16[24,16,512]{2,1,0:T(8,128)(2,1)S(1)}, bf16[24,16,512]{2,1,0:T(8,128)(2,1)}, u32[]{:S(2)}, u32[]{:S(2)}) collective-permute-start(bf16[24,16,512]{2,1,0:T(8,128)(2,1)S(1)} %add.156), channel_id=1, source_target_pairs={{0,4},{8,12},{16,20},{24,28},{1,5},{9,13},{17,21},{25,29},{2,6},{1... | collective-permute-start | bytes 1179656 | tf_op jit(solution)/shard_map/ppermute | solution.py:79
  127.6 22.7 %collective-permute-start.13 = (bf16[24,16,512]{2,1,0:T(8,128)(2,1)S(1)}, bf16[24,16,512]{2,1,0:T(8,128)(2,1)}, u32[]{:S(2)}, u32[]{:S(2)}) collective-permute-start(bf16[24,16,512]{2,1,0:T(8,128)(2,1)S(1)} %add.159), channel_id=1, source_target_pairs={{28,24},{20,16},{12,8},{4,0},{29,25},{21,17},{13,9},{5,1},{30,26},... | collective-permute-start | bytes 1179656 | tf_op jit(solution)/shard_map/ppermute | solution.py:79
  129.1 22.4 %collective-permute-start.16 = (bf16[24,16,512]{2,1,0:T(8,128)(2,1)S(1)}, bf16[24,16,512]{2,1,0:T(8,128)(2,1)}, u32[]{:S(2)}, u32[]{:S(2)}) collective-permute-start(bf16[24,16,512]{2,1,0:T(8,128)(2,1)S(1)} %add.162), channel_id=1, source_target_pairs={{28,24},{20,16},{12,8},{4,0},{29,25},{21,17},{13,9},{5,1},{30,26},... | collective-permute-start | bytes 1179656 | tf_op jit(solution)/shard_map/ppermute | solution.py:79
  191.5 1.7 copy-start.1
  226.4 13.8 %copy-start.2 = (bf16[48,32,512]{1,0,2:T(8,128)(2,1)S(1)}, bf16[48,32,512]{1,0,2:T(8,128)(2,1)}, u32[]{:S(2)}) copy-start(bf16[48,32,512]{1,0,2:T(8,128)(2,1)} %copy.38) | copy-start | bytes 4718596
  240.2 30.2 %slice-start = ((s8[6291456]{0:T(1024)(128)(4,1)}), s8[4194304]{0:T(1024)(128)(4,1)S(1)}, s32[]{:S(2)}) async-start(s8[6291456]{0:T(1024)(128)(4,1)} %bitcast.32), calls=%async_computation.1 | async-start | bytes 8388608
  246.0 24.4 %slice-start.1 = ((s8[6291456]{0:T(1024)(128)(4,1)}), s8[2097152]{0:T(1024)(128)(4,1)S(1)}, s32[]{:S(2)}) async-start(s8[6291456]{0:T(1024)(128)(4,1)} %bitcast.32), calls=%async_computation.2 | async-start | bytes 4194304
  270.3 30.4 %collective-permute-start.18 = (bf16[16,128,256]{2,1,0:T(8,128)(2,1)S(1)}, bf16[16,128,256]{2,1,0:T(8,128)(2,1)S(1)}, u32[]{:S(2)}, u32[]{:S(2)}) collective-permute-start(bf16[16,128,256]{2,1,0:T(8,128)(2,1)S(1)} %dynamic-slice_convert_fusion), channel_id=1, source_target_pairs={{0,1},{1,0},{2,3},{3,2},{4,5},{5,4},{6,7},{7,6},{8,9},{9,8},{10,11... | collective-permute-start | bytes 3145736 | tf_op jit(solution)/shard_map/ppermute | solution.py:228
  300.1 2.8 collective-permute-start.17
  300.9 25.2 %collective-permute-start.19 = (bf16[16,128,256]{2,1,0:T(8,128)(2,1)S(1)}, bf16[16,128,256]{2,1,0:T(8,128)(2,1)S(1)}, u32[]{:S(2)}, u32[]{:S(2)}) collective-permute-start(bf16[16,128,256]{2,1,0:T(8,128)(2,1)S(1)} %add_convert_fusion), channel_id=1, source_target_pairs={{0,2},{1,3},{2,0},{3,1},{4,6},{5,7},{6,4},{7,5},{8,10},{9,11},{10,... | collective-permute-start | bytes 3145736 | tf_op jit(solution)/shard_map/ppermute | solution.py:232
Sparse Core Ops, SparseCore 0:
  74.0 106.8 all-reduce.1

commit v3 on v2

--- a/solution.py
+++ b/solution.py
@@ -83,13 +83,21 @@
 
 def stack_kernel(src_re, src_im, chan_re, chan_im, high_ref, low_ref, out_ref, cross):
     step = pl.program_id(0)
-    bins, segs, rows = src_re.shape
+    bins, segs, src_count = src_re.shape
+    rows = 2 * src_count
     total_bins = high_ref.shape[0] // 2
     out_rows = rows // 2
     contract = (((0,), (0,)), ((), ()))
 
     for place in range(bins):
-        left = jnp.concatenate([src_re[place], src_im[place]], axis=0)
+        real, imag = src_re[place], src_im[place]
+        left = jnp.concatenate(
+            [
+                jnp.concatenate([real, imag], axis=1),
+                jnp.concatenate([imag, -real], axis=1),
+            ],
+            axis=0,
+        )
         right = jnp.concatenate([chan_re[place], chan_im[place]], axis=0)
         first = pl.multiple_of((step * bins + place) * rows, rows)
         cross[pl.ds(first, rows), :] = lax.dot_general(
@@ -113,11 +121,12 @@
             out_ref[row] = total
             return carry
 
-        lax.fori_loop(0, out_rows, one, 0)
+        lax.fori_loop(0, out_rows, one, 0, unroll=2)
 
 
 def stack_lags(sources, channels, inverse):
-    length, segs, rows = sources.shape
+    length, segs, src_count = sources.shape
+    rows = 2 * src_count
     chans = channels.shape[2]
     lags = inverse.shape[1]
     step = 32
@@ -129,8 +138,8 @@
         stack_kernel,
         grid=(steps,),
         in_specs=[
-            pl.BlockSpec((step, segs, rows), lambda i: (i, 0, 0)),
-            pl.BlockSpec((step, segs, rows), lambda i: (i + steps, 0, 0)),
+            pl.BlockSpec((step, segs, src_count), lambda i: (i, 0, 0)),
+            pl.BlockSpec((step, segs, src_count), lambda i: (i + steps, 0, 0)),
             pl.BlockSpec((step, segs, chans), lambda i: (i, 0, 0)),
             pl.BlockSpec((step, segs, chans), lambda i: (i + steps, 0, 0)),
             whole,
@@ -139,7 +148,7 @@
         out_specs=pl.BlockSpec((rows // 2, chans, lags), lambda i: (0, 0, 0)),
         out_shape=jax.ShapeDtypeStruct((rows // 2, chans, lags), jnp.float32),
         scratch_shapes=[pltpu.VMEM((length // 2 * rows, chans), jnp.float32)],
-        compiler_params=pltpu.CompilerParams(vmem_limit_bytes=40 << 20),
+        compiler_params=pltpu.CompilerParams(vmem_limit_bytes=48 << 20),
         cost_estimate=pl.CostEstimate(
             flops=20_000_000_000, bytes_accessed=16_000_000, transcendentals=0
         ),
@@ -204,34 +213,25 @@
 
     whitened = whiten(displacement, table)
     sources = whiten(chosen, table)
-    swapped = jnp.concatenate([sources[:, :, bin_count:], -sources[:, :, :bin_count]], axis=2)
     channels = jnp.transpose(whitened, (2, 0, 1))
-
     inverse = lag_table(length, bin_count, bin_count)
     day = lax.axis_index("day")
     day_count = lax.axis_size("day")
-    half_count = day_count // 2
     part = source_count // day_count
     near = [(i, i ^ 1) for i in range(day_count)]
     far = [(i, i ^ 2) for i in range(day_count)]
 
-    def lagged(first):
-        one = lax.dynamic_slice_in_dim(sources, first, half_count * part, axis=1)
-        two = lax.dynamic_slice_in_dim(swapped, first, half_count * part, axis=1)
-        both = jnp.transpose(jnp.concatenate([one, two], axis=1), (2, 0, 1))
-        return stack_lags(both, channels, inverse)
-
-    def pair_sum(value):
-        core = day % 2
-        keep = lax.dynamic_slice_in_dim(value, core * part, part, axis=0)
-        give = lax.dynamic_slice_in_dim(value, (1 - core) * part, part, axis=0)
-        return keep + lax.ppermute(give.astype(jnp.bfloat16), "day", near).astype(jnp.float32)
-
-    upper = day // 2
-    other = pair_sum(lagged((1 - upper) * half_count * part))
-    came = lax.ppermute(other.astype(jnp.bfloat16), "day", far)
-    own = pair_sum(lagged(upper * half_count * part))
-    return (own + came.astype(jnp.float32)) * (1.0 / (seg_count * day_count))
+    lags = stack_lags(jnp.transpose(sources, (2, 0, 1)), channels, inverse)
+    lags = lags.reshape(day_count // 2, 2, part, chan_count, -1)
+
+    def pair_sum(value, place, axis, pairs):
+        keep = lax.dynamic_index_in_dim(value, place, axis, False)
+        give = lax.dynamic_index_in_dim(value, 1 - place, axis, False)
+        came = lax.ppermute(give.astype(jnp.bfloat16), "day", pairs)
+        return keep + came.astype(jnp.float32)
+
+    total = pair_sum(pair_sum(lags, day % 2, 1, near), day // 2, 0, far)
+    return total * (1.0 / (seg_count * day_count))
 
 
 def solution(mesh):

time: 336 us -> 286 us (0.85)
  other arithmetic: 62.3 us -> 39.1 us
  starting transfers between devices: 35.1 us -> 50.9 us
  Pallas kernels: 48.1 us -> 33.3 us
  local copies, waits for them, and re-layouts: 44.1 us -> 30.3 us
  waiting for transfers between devices: 110 us -> 96.4 us
    unnamed x22 -> x12, local copies, waits for them, and re-layouts: 27 us -> 5.71 us
    pallas_call x2 -> x1, Pallas kernels: 48.1 us -> 33.3 us  [stack_lags(): pl.pallas_call(stack_kernel, grid=(steps,), in_specs=[pl.BlockSpec((step,...]
    concatenate x1 -> x0, other arithmetic: 13.8 us -> none  [per_device(): jnp.concatenate([sources[:, :, bin_count:], -sources[:, :, :bin_count]],...]
    ppermute x15, waiting for transfers between devices: 58.3 us -> 44.6 us  [spread(): block = block + lax.ppermute(block, axis, pairs)]
    ppermute x15, starting transfers between devices: 29.5 us -> 42.5 us  [spread(): block = block + lax.ppermute(block, axis, pairs)]
    transpose x2 -> x0, other arithmetic: 11.3 us -> none  [lagged(): both = jnp.transpose(jnp.concatenate([one, two], axis=1), (2, 0, 1))]
    reshape x1 -> x2, local copies, waits for them, and re-layouts: 9.07 us -> 17.7 us  [whiten(): return whitened.reshape(segs, rows, length)]
    psum x1, waiting for transfers between devices: 28.3 us -> 23.9 us  [per_device(): middle = lax.psum(offered[:, block_src:-block_src], 'fibre')]
  transfers between devices with their start and end apart: 21 -> 20, of which waited for: 9 -> 8; matrix products, arithmetic and copies ran while one was open for 13% -> 14% of each run, Pallas kernels for 7% -> 0%
where the time goes in v3:
time: 286 us; the launch traced here: 285 us
  waiting for transfers between devices  96.4 us (34%)
  starting transfers between devices  50.9 us (18%)
  other arithmetic  39.1 us (14%)
  Pallas kernels  33.3 us (12%)
  local copies, waits for them, and re-layouts  30.3 us (11%)
  matrix products  21 us (7%)
  between operations  13.8 us (5%)
    ppermute x15, waiting for transfers between devices, spread(): block = block + lax.ppermute(block, axis, pairs)  44.6 us
    ppermute x15, starting transfers between devices, spread(): block = block + lax.ppermute(block, axis, pairs)  42.5 us
    pallas_call x1, Pallas kernels, stack_lags(): pl.pallas_call(stack_kernel, grid=(steps,), in_specs=[pl.BlockSpec((step,...  33.3 us
    ppermute x2, waiting for transfers between devices, pair_sum(): came = lax.ppermute(give.astype(jnp.bfloat16), 'day', pairs)  28 us
    psum x1, waiting for transfers between devices, per_device(): middle = lax.psum(offered[:, block_src:-block_src], 'fibre')  23.9 us
    reshape x2, local copies, waits for them, and re-layouts, whiten(): return whitened.reshape(segs, rows, length)  17.7 us
    convert_element_type x2, other arithmetic, whiten(): (spectra * jnp.concatenate([inv_amp, inv_amp], axis=1)).astype(jnp.bfloat16)  15.2 us
    dot_general x2, matrix products, whiten(): jnp.dot(displacement.reshape(-1, length), table, preferred_element_type=j...  7.3 us
  transfers between devices with their start and end apart: 20, of which 8 were waited for; matrix products, arithmetic and copies ran while one was open for 14% of the time, Pallas kernels for 0%

profile of v3, /device:TPU:0, one launch (start us, length us, event | category | flops | bytes accessed | tf_op | source)
XLA Modules:
  0.0 284.9 jit_solution(13244159190176832323)
XLA Ops:
  8.0 5.0 %fusion.1 = bf16[48,128,512]{2,1,0:T(8,128)(2,1)S(1)} fusion(bf16[1,48,128,512]{3,2,1,0:T(8,128)(2,1)} %param.5, f32[128]{0:T(128)S(1)} %convert_multiply_fusion.1), kind=kLoop, calls=%fused_computation.3 | loop fusion | flops 9437184 | bytes 12583424 | tf_op jit(solution)/shard_map/convert_element_type | solution.py:170
  13.0 2.7 copy-done.4
  16.1 5.9 %collective-permute-start.2 = (f32[48,512]{1,0:T(8,128)S(1)}, f32[48,512]{1,0:T(8,128)S(1)}, u32[]{:S(2)}, u32[]{:S(2)}) collective-permute-start(f32[48,512]{1,0:T(8,128)S(1)} %broadcast_select_fusion), channel_id=1, source_target_pairs={{0,16},{1,17},{2,18},{3,19}} | collective-permute-start | bytes 294920 | tf_op jit(solution)/shard_map/ppermute | solution.py:79
  22.1 1.5 fusion.78
  24.9 5.4 %collective-permute-start = (bf16[48,16,512]{2,1,0:T(8,128)(2,1)S(1)}, bf16[48,16,512]{2,1,0:T(8,128)(2,1)}, u32[]{:S(2)}, u32[]{:S(2)}) collective-permute-start(bf16[48,16,512]{2,1,0:T(8,128)(2,1)S(1)} %get-tuple-element.5), channel_id=1, source_target_pairs={{0,4},{4,8},{8,12},{12,16},{16,20},{20,24},{24,28},{1,5},{5,9},{9,... | collective-permute-start | bytes 2359304 | tf_op jit(solution)/shard_map/ppermute | solution.py:17
  30.4 2.3 multiply_convert_fusion.1
  35.4 2.2 collective-permute-done.3
  38.9 20.9 %collective-permute-done.4 = f32[48,512]{1,0:T(8,128)S(1)} collective-permute-done((f32[48,512]{1,0:T(8,128)S(1)}, f32[48,512]{1,0:T(8,128)S(1)}, u32[]{:S(2)}, u32[]{:S(2)}) %collective-permute-start.4) | collective-permute-done | bytes 98336 | tf_op jit(solution)/shard_map/ppermute | solution.py:79
  59.8 4.5 %multiply_convert_fusion = bf16[48,512,128]{1,2,0:T(8,128)(2,1)S(1)} fusion(f32[48,512]{1,0:T(8,128)S(1)} %add.145, bf16[48,16,512]{2,1,0:T(8,128)(2,1)} %collective-permute-done.1, bf16[48,128,512]{2,1,0:T(8,128)(2,1)} %copy-done.4, bf16[48,16,512]{2,1,0:T(8,128)(2,1)} %collective-permute-done), kind=kOutput, calls=%fused_computation.4 | convolution fusion | flops 1039847424 | bytes 14254080 | tf_op jit(solution)/shard_map/ck,gkt->gct/dot_general | solution.py:183
  69.4 4.5 %collective-permute-start.5 = (bf16[24,16,512]{2,1,0:T(8,128)(2,1)}, bf16[24,16,512]{2,1,0:T(8,128)(2,1)S(1)}, u32[]{:S(2)}, u32[]{:S(2)}) collective-permute-start(bf16[24,16,512]{2,1,0:T(8,128)(2,1)} %get-tuple-element.11), channel_id=1, source_target_pairs={{0,16},{1,17},{2,18},{3,19}} | collective-permute-start | bytes 1179656 | tf_op jit(solution)/shard_map/ppermute | solution.py:79
  77.4 5.5 %fusion.43 = f32[6144,512]{1,0:T(8,128)S(1)} fusion(bf16[6144,512]{1,0:T(8,128)(2,1)} %bitcast.40, bf16[512,256]{1,0:T(8,128)(2,1)S(1)} %get-tuple-element.19, bf16[512,256]{1,0:T(8,128)(2,1)S(1)} %get-tuple-element.20), kind=kOutput, calls=%fused_computation.65 | convolution fusion | flops 3222274048 | bytes 19398656 | tf_op jit(solution)/shard_map/dot_general | solution.py:63
  84.4 15.8 %collective-permute-done.8 = bf16[24,16,512]{2,1,0:T(8,128)(2,1)S(1)} collective-permute-done((bf16[24,16,512]{2,1,0:T(8,128)(2,1)S(1)}, bf16[24,16,512]{2,1,0:T(8,128)(2,1)S(1)}, u32[]{:S(2)}, u32[]{:S(2)}) %collective-permute-start.8) | collective-permute-done | bytes 393248 | tf_op jit(solution)/shard_map/ppermute | solution.py:79
  105.6 3.7 %fusion.10 = f32[6144,256]{1,0:T(8,128)} fusion(f32[6144,256]{1,0:T(8,128)S(1)} %fusion.26, f32[256]{0:T(256)S(1)} %convert_reduce_fusion, f32[6144,512]{1,0:T(8,128)S(1)} %fusion.43), kind=kOutput, calls=%fused_computation.14 | convolution fusion | flops 821231616 | bytes 25166848 | tf_op jit(solution)/shard_map/dot_general | solution.py:44
  112.2 5.3 %collective-permute-done.9 = bf16[24,16,512]{2,1,0:T(8,128)(2,1)S(1)} collective-permute-done((bf16[24,16,512]{2,1,0:T(8,128)(2,1)S(1)}, bf16[24,16,512]{2,1,0:T(8,128)(2,1)S(1)}, u32[]{:S(2)}, u32[]{:S(2)}) %collective-permute-start.9) | collective-permute-done | bytes 393248 | tf_op jit(solution)/shard_map/ppermute | solution.py:79
  117.6 17.3 %collective-permute-start.10 = (bf16[24,16,512]{2,1,0:T(8,128)(2,1)S(1)}, bf16[24,16,512]{2,1,0:T(8,128)(2,1)}, u32[]{:S(2)}, u32[]{:S(2)}) collective-permute-start(bf16[24,16,512]{2,1,0:T(8,128)(2,1)S(1)} %add.152), channel_id=1, source_target_pairs={{0,4},{8,12},{16,20},{24,28},{1,5},{9,13},{17,21},{25,29},{2,6},{1... | collective-permute-start | bytes 1179656 | tf_op jit(solution)/shard_map/ppermute | solution.py:79
  135.0 2.0 collective-permute-start.7
  137.0 9.7 %fusion = bf16[6144,512]{1,0:T(8,128)(2,1)} fusion(f32[6144,512]{1,0:T(8,128)S(1)} %fusion.43, f32[6144,256]{1,0:T(8,128)} %fusion.10), kind=kLoop, calls=%fused_computation.1 | loop fusion | flops 9437184 | bytes 25165824 | tf_op jit(solution)/shard_map/convert_element_type | solution.py:70
  146.8 9.1 %copy.31 = bf16[48,128,512]{1,0,2:T(8,128)(2,1)} copy(bf16[48,128,512]{2,1,0:T(8,128)(2,1)} %bitcast.41) | data formatting | bytes 12582912 | tf_op jit(solution)/shard_map/reshape | solution.py:71
  159.4 23.9 %all-reduce.2.cloned.1.call-done = bf16[48,32,512]{2,1,0:T(8,128)(2,1)} async-done(((bf16[48,32,512]{2,1,0:T(8,128)(2,1)}), bf16[48,32,512]{2,1,0:T(8,128)(2,1)}) %all-reduce.2.cloned.1.call-update) | async-done | bytes 1572880 | tf_op jit(solution)/shard_map/psum | solution.py:197
  183.3 1.6 maximum_maximum_fusion
  184.9 1.8 fusion.44
  187.3 2.6 fusion.19
  189.9 5.5 %fusion.12 = bf16[3072,512]{1,0:T(8,128)(2,1)} fusion(f32[3072,512]{1,0:T(8,128)S(1)} %fusion.44, f32[3072,256]{1,0:T(8,128)} %fusion.19), kind=kLoop, calls=%fused_computation.19 | loop fusion | flops 4718592 | bytes 12582912 | tf_op jit(solution)/shard_map/convert_element_type | solution.py:70
  195.4 8.6 %copy.22 = bf16[48,64,512]{1,0,2:T(8,128)(2,1)} copy(bf16[48,64,512]{2,1,0:T(8,128)(2,1)} %bitcast.43) | data formatting | bytes 6291456 | tf_op jit(solution)/shard_map/reshape | solution.py:71
  204.0 33.3 %shard_map.55 = f32[64,128,256]{2,1,0:T(8,128)} custom-call(bf16[512,48,64]{2,1,0:T(8,128)(2,1)} %bitcast.46, bf16[512,48,64]{2,1,0:T(8,128)(2,1)} %bitcast.47, bf16[512,48,128]{2,1,0:T(8,128)(2,1)} %bitcast.44, bf16[512,48,128]{2,1,0:T(8,128)(2,1)} %bitcast.45, bf16[512,256]{1,0:T(8,128)(2,1)S(1)} %fusion.42.high_ref, ...), custom_call_target="tpu_custom_call" | custom-call | flops 20000000000 | bytes 16000000 | tf_op jit(solution)/shard_map/pallas_call | solution.py:137
  237.3 2.5 fusion.23
  239.9 4.2 %collective-permute-done.17 = bf16[2,16,128,256]{3,2,1,0:T(8,128)(2,1)} collective-permute-done((bf16[2,16,128,256]{3,2,1,0:T(8,128)(2,1)S(1)}, bf16[2,16,128,256]{3,2,1,0:T(8,128)(2,1)}, u32[]{:S(2)}, u32[]{:S(2)}) %collective-permute-start.17) | collective-permute-done | bytes 2097184 | tf_op jit(solution)/shard_map/ppermute | solution.py:230
  244.2 3.4 %bitcast_add_fusion = f32[2,16,128,256]{3,2,1,0:T(8,128)S(1)} fusion(bf16[2,16,128,256]{3,2,1,0:T(8,128)(2,1)} %collective-permute-done.17, f32[2,2,16,128,256]{4,3,2,1,0:T(8,128)} %bitcast.49, s32[]{:T(128)S(6)} %select_n.97), kind=kLoop, calls=%fused_computation.24 | loop fusion | flops 2097152 | bytes 10485764 | tf_op jit(solution)/shard_map/add | solution.py:231
  247.6 1.9 copy-done.3
  249.6 1.5 collective-permute-start.18
  251.2 23.7 %collective-permute-done.18 = bf16[16,128,256]{2,1,0:T(8,128)(2,1)S(1)} collective-permute-done((bf16[16,128,256]{2,1,0:T(8,128)(2,1)S(1)}, bf16[16,128,256]{2,1,0:T(8,128)(2,1)S(1)}, u32[]{:S(2)}, u32[]{:S(2)}) %collective-permute-start.18) | collective-permute-done | bytes 1048608 | tf_op jit(solution)/shard_map/ppermute | solution.py:230
  274.9 3.2 %fusion.24 = f32[16,128,256]{2,1,0:T(8,128)} fusion(bf16[16,128,256]{2,1,0:T(8,128)(2,1)S(1)} %collective-permute-done.18, f32[2,16,128,256]{3,2,1,0:T(8,128)} %copy-done.3, s32[]{:T(128)S(6)} %select_n.100), kind=kLoop, calls=%fused_computation.37 | loop fusion | flops 1572864 | bytes 5242884 | tf_op jit(solution)/shard_map/mul | solution.py:234
  (71 shorter events, 30.0 us)
Async XLA Ops:
  6.5 176.7 %all-reduce.2.cloned.1.call-start = ((), (), s32[]{:S(2)}) async-start(), calls=%async_computation | async-start | bytes 3145728 | tf_op jit(solution)/shard_map/psum | solution.py:197
  8.0 25.8 %copy-start.5 = (s32[4,16]{1,0:T(4,128)S(1)}, s32[4,16]{1,0:T(4,128)}, u32[]{:S(2)}) copy-start(s32[4,16]{1,0:T(4,128)} %param.9) | copy-start | bytes 772
  13.0 2.7 copy-start.4
  16.1 17.9 %collective-permute-start.2 = (f32[48,512]{1,0:T(8,128)S(1)}, f32[48,512]{1,0:T(8,128)S(1)}, u32[]{:S(2)}, u32[]{:S(2)}) collective-permute-start(f32[48,512]{1,0:T(8,128)S(1)} %broadcast_select_fusion), channel_id=1, source_target_pairs={{0,16},{1,17},{2,18},{3,19}} | collective-permute-start | bytes 294920 | tf_op jit(solution)/shard_map/ppermute | solution.py:79
  23.6 36.2 %collective-permute-start.1 = (bf16[48,16,512]{2,1,0:T(8,128)(2,1)S(1)}, bf16[48,16,512]{2,1,0:T(8,128)(2,1)}, u32[]{:S(2)}, u32[]{:S(2)}) collective-permute-start(bf16[48,16,512]{2,1,0:T(8,128)(2,1)S(1)} %get-tuple-element.6), channel_id=1, source_target_pairs={{4,0},{8,4},{12,8},{16,12},{20,16},{24,20},{28,24},{5,1},{9,5},{13... | collective-permute-start | bytes 2359304 | tf_op jit(solution)/shard_map/ppermute | solution.py:18
  24.9 34.9 %collective-permute-start = (bf16[48,16,512]{2,1,0:T(8,128)(2,1)S(1)}, bf16[48,16,512]{2,1,0:T(8,128)(2,1)}, u32[]{:S(2)}, u32[]{:S(2)}) collective-permute-start(bf16[48,16,512]{2,1,0:T(8,128)(2,1)S(1)} %get-tuple-element.5), channel_id=1, source_target_pairs={{0,4},{4,8},{8,12},{12,16},{16,20},{20,24},{24,28},{1,5},{5,9},{9,... | collective-permute-start | bytes 2359304 | tf_op jit(solution)/shard_map/ppermute | solution.py:17
  34.0 3.5 %collective-permute-start.3 = (f32[48,512]{1,0:T(8,128)S(1)}, f32[48,512]{1,0:T(8,128)S(1)}, u32[]{:S(2)}, u32[]{:S(2)}) collective-permute-start(f32[48,512]{1,0:T(8,128)S(1)} %fusion.82), channel_id=1, source_target_pairs={{0,8},{16,24},{1,9},{17,25},{2,10},{18,26},{3,11},{19,27}} | collective-permute-start | bytes 294920 | tf_op jit(solution)/shard_map/ppermute | solution.py:79
  37.5 22.2 %collective-permute-start.4 = (f32[48,512]{1,0:T(8,128)S(1)}, f32[48,512]{1,0:T(8,128)S(1)}, u32[]{:S(2)}, u32[]{:S(2)}) collective-permute-start(f32[48,512]{1,0:T(8,128)S(1)} %add.144), channel_id=1, source_target_pairs={{0,4},{8,12},{16,20},{24,28},{1,5},{9,13},{17,21},{25,29},{2,6},{1... | collective-permute-start | bytes 294920 | tf_op jit(solution)/shard_map/ppermute | solution.py:79
  64.4 2.8 copy-start
  65.6 2.6 copy-start.1
  69.4 15.0 %collective-permute-start.5 = (bf16[24,16,512]{2,1,0:T(8,128)(2,1)}, bf16[24,16,512]{2,1,0:T(8,128)(2,1)S(1)}, u32[]{:S(2)}, u32[]{:S(2)}) collective-permute-start(bf16[24,16,512]{2,1,0:T(8,128)(2,1)} %get-tuple-element.11), channel_id=1, source_target_pairs={{0,16},{1,17},{2,18},{3,19}} | collective-permute-start | bytes 1179656 | tf_op jit(solution)/shard_map/ppermute | solution.py:79
  73.9 26.3 %collective-permute-start.8 = (bf16[24,16,512]{2,1,0:T(8,128)(2,1)S(1)}, bf16[24,16,512]{2,1,0:T(8,128)(2,1)S(1)}, u32[]{:S(2)}, u32[]{:S(2)}) collective-permute-start(bf16[24,16,512]{2,1,0:T(8,128)(2,1)S(1)} %get-tuple-element.14), channel_id=1, source_target_pairs={{0,16},{1,17},{2,18},{3,19}} | collective-permute-start | bytes 1179656 | tf_op jit(solution)/shard_map/ppermute | solution.py:79
  75.2 24.9 %collective-permute-start.11 = (bf16[24,16,512]{2,1,0:T(8,128)(2,1)S(1)}, bf16[24,16,512]{2,1,0:T(8,128)(2,1)S(1)}, u32[]{:S(2)}, u32[]{:S(2)}) collective-permute-start(bf16[24,16,512]{2,1,0:T(8,128)(2,1)S(1)} %get-tuple-element.13), channel_id=1, source_target_pairs={{28,12},{29,13},{30,14},{31,15}} | collective-permute-start | bytes 1179656 | tf_op jit(solution)/shard_map/ppermute | solution.py:79
  75.9 24.2 %collective-permute-start.14 = (bf16[24,16,512]{2,1,0:T(8,128)(2,1)S(1)}, bf16[24,16,512]{2,1,0:T(8,128)(2,1)}, u32[]{:S(2)}, u32[]{:S(2)}) collective-permute-start(bf16[24,16,512]{2,1,0:T(8,128)(2,1)S(1)} %get-tuple-element.12), channel_id=1, source_target_pairs={{28,12},{29,13},{30,14},{31,15}} | collective-permute-start | bytes 1179656 | tf_op jit(solution)/shard_map/ppermute | solution.py:79
  82.9 17.3 %copy-start.2 = (bf16[48,64,512]{2,1,0:T(8,128)(2,1)S(1)}, bf16[48,64,512]{2,1,0:T(8,128)(2,1)}, u32[]{:S(2)}) copy-start(bf16[48,64,512]{2,1,0:T(8,128)(2,1)} %copy-done.1) | copy-start | bytes 9437188
  101.4 7.9 %collective-permute-start.15 = (bf16[24,16,512]{2,1,0:T(8,128)(2,1)S(1)}, bf16[24,16,512]{2,1,0:T(8,128)(2,1)S(1)}, u32[]{:S(2)}, u32[]{:S(2)}) collective-permute-start(bf16[24,16,512]{2,1,0:T(8,128)(2,1)S(1)} %get-tuple-element.10), channel_id=1, source_target_pairs={{28,20},{12,4},{29,21},{13,5},{30,22},{14,6},{31,23},{15,7}} | collective-permute-start | bytes 1179656 | tf_op jit(solution)/shard_map/ppermute | solution.py:79
  102.1 8.6 %collective-permute-start.12 = (bf16[24,16,512]{2,1,0:T(8,128)(2,1)S(1)}, bf16[24,16,512]{2,1,0:T(8,128)(2,1)S(1)}, u32[]{:S(2)}, u32[]{:S(2)}) collective-permute-start(bf16[24,16,512]{2,1,0:T(8,128)(2,1)S(1)} %get-tuple-element.9), channel_id=1, source_target_pairs={{28,20},{12,4},{29,21},{13,5},{30,22},{14,6},{31,23},{15,7}} | collective-permute-start | bytes 1179656 | tf_op jit(solution)/shard_map/ppermute | solution.py:79
  102.8 14.7 %collective-permute-start.9 = (bf16[24,16,512]{2,1,0:T(8,128)(2,1)S(1)}, bf16[24,16,512]{2,1,0:T(8,128)(2,1)S(1)}, u32[]{:S(2)}, u32[]{:S(2)}) collective-permute-start(bf16[24,16,512]{2,1,0:T(8,128)(2,1)S(1)} %get-tuple-element.8), channel_id=1, source_target_pairs={{0,8},{16,24},{1,9},{17,25},{2,10},{18,26},{3,11},{19,27}} | collective-permute-start | bytes 1179656 | tf_op jit(solution)/shard_map/ppermute | solution.py:79
  104.1 30.7 %collective-permute-start.6 = (bf16[24,16,512]{2,1,0:T(8,128)(2,1)S(1)}, bf16[24,16,512]{2,1,0:T(8,128)(2,1)S(1)}, u32[]{:S(2)}, u32[]{:S(2)}) collective-permute-start(bf16[24,16,512]{2,1,0:T(8,128)(2,1)S(1)} %get-tuple-element.7), channel_id=1, source_target_pairs={{0,8},{16,24},{1,9},{17,25},{2,10},{18,26},{3,11},{19,27}} | collective-permute-start | bytes 1179656 | tf_op jit(solution)/shard_map/ppermute | solution.py:79
  109.4 46.4 %collective-permute-start.16 = (bf16[24,16,512]{2,1,0:T(8,128)(2,1)S(1)}, bf16[24,16,512]{2,1,0:T(8,128)(2,1)S(1)}, u32[]{:S(2)}, u32[]{:S(2)}) collective-permute-start(bf16[24,16,512]{2,1,0:T(8,128)(2,1)S(1)} %add.158), channel_id=1, source_target_pairs={{28,24},{20,16},{12,8},{4,0},{29,25},{21,17},{13,9},{5,1},{30,26},... | collective-permute-start | bytes 1179656 | tf_op jit(solution)/shard_map/ppermute | solution.py:79
  110.9 45.1 %collective-permute-start.13 = (bf16[24,16,512]{2,1,0:T(8,128)(2,1)S(1)}, bf16[24,16,512]{2,1,0:T(8,128)(2,1)}, u32[]{:S(2)}, u32[]{:S(2)}) collective-permute-start(bf16[24,16,512]{2,1,0:T(8,128)(2,1)S(1)} %add.155), channel_id=1, source_target_pairs={{28,24},{20,16},{12,8},{4,0},{29,25},{21,17},{13,9},{5,1},{30,26},... | collective-permute-start | bytes 1179656 | tf_op jit(solution)/shard_map/ppermute | solution.py:79
  117.6 39.5 %collective-permute-start.10 = (bf16[24,16,512]{2,1,0:T(8,128)(2,1)S(1)}, bf16[24,16,512]{2,1,0:T(8,128)(2,1)}, u32[]{:S(2)}, u32[]{:S(2)}) collective-permute-start(bf16[24,16,512]{2,1,0:T(8,128)(2,1)S(1)} %add.152), channel_id=1, source_target_pairs={{0,4},{8,12},{16,20},{24,28},{1,5},{9,13},{17,21},{25,29},{2,6},{1... | collective-permute-start | bytes 1179656 | tf_op jit(solution)/shard_map/ppermute | solution.py:79
  135.0 23.3 %collective-permute-start.7 = (bf16[24,16,512]{2,1,0:T(8,128)(2,1)S(1)}, bf16[24,16,512]{2,1,0:T(8,128)(2,1)}, u32[]{:S(2)}, u32[]{:S(2)}) collective-permute-start(bf16[24,16,512]{2,1,0:T(8,128)(2,1)S(1)} %add.149), channel_id=1, source_target_pairs={{0,4},{8,12},{16,20},{24,28},{1,5},{9,13},{17,21},{25,29},{2,6},{1... | collective-permute-start | bytes 1179656 | tf_op jit(solution)/shard_map/ppermute | solution.py:79
  239.8 4.4 %collective-permute-start.17 = (bf16[2,16,128,256]{3,2,1,0:T(8,128)(2,1)S(1)}, bf16[2,16,128,256]{3,2,1,0:T(8,128)(2,1)}, u32[]{:S(2)}, u32[]{:S(2)}) collective-permute-start(bf16[2,16,128,256]{3,2,1,0:T(8,128)(2,1)S(1)} %fusion.23), channel_id=1, source_target_pairs={{0,1},{1,0},{2,3},{3,2},{4,5},{5,4},{6,7},{7,6},{8,9},{9,8},{10,11... | collective-permute-start | bytes 6291464 | tf_op jit(solution)/shard_map/ppermute | solution.py:230
  247.6 1.9 copy-start.3
  249.6 25.3 %collective-permute-start.18 = (bf16[16,128,256]{2,1,0:T(8,128)(2,1)S(1)}, bf16[16,128,256]{2,1,0:T(8,128)(2,1)S(1)}, u32[]{:S(2)}, u32[]{:S(2)}) collective-permute-start(bf16[16,128,256]{2,1,0:T(8,128)(2,1)S(1)} %fusion.30), channel_id=1, source_target_pairs={{0,2},{1,3},{2,0},{3,1},{4,6},{5,7},{6,4},{7,5},{8,10},{9,11},{10,... | collective-permute-start | bytes 3145736 | tf_op jit(solution)/shard_map/ppermute | solution.py:230
Sparse Core Ops, SparseCore 0:
  77.5 105.7 all-reduce.1

commit v4 on v3

--- a/solution.py
+++ b/solution.py
@@ -81,16 +81,19 @@
     return block
 
 
-def stack_kernel(src_re, src_im, chan_re, chan_im, high_ref, low_ref, out_ref, cross):
+def stack_kernel(end_re, end_im, mid_re, mid_im, chan_re, chan_im, high_ref, low_ref, out_ref, cross):
     step = pl.program_id(0)
-    bins, segs, src_count = src_re.shape
+    bins, segs, end_count = end_re.shape
+    src_count = end_count + mid_re.shape[2]
+    block = end_count // 2
     rows = 2 * src_count
     total_bins = high_ref.shape[0] // 2
     out_rows = rows // 2
     contract = (((0,), (0,)), ((), ()))
 
     for place in range(bins):
-        real, imag = src_re[place], src_im[place]
+        real = jnp.concatenate([end_re[place], mid_re[place]], axis=1)
+        imag = jnp.concatenate([end_im[place], mid_im[place]], axis=1)
         left = jnp.concatenate(
             [
                 jnp.concatenate([real, imag], axis=1),
@@ -118,15 +121,17 @@
                         lhs, rhs[keep, :], contract, preferred_element_type=jnp.float32
                     )
                     total = term if total is None else total + term
-            out_ref[row] = total
+            late = jnp.where(row < end_count, row + src_count - end_count, row - block)
+            out_ref[jnp.where(row < block, row, late)] = total
             return carry
 
         lax.fori_loop(0, out_rows, one, 0, unroll=2)
 
 
-def stack_lags(sources, channels, inverse):
-    length, segs, src_count = sources.shape
-    rows = 2 * src_count
+def stack_lags(ends, middle, channels, inverse):
+    length, segs, end_count = ends.shape
+    mid_count = middle.shape[2]
+    rows = 2 * (end_count + mid_count)
     chans = channels.shape[2]
     lags = inverse.shape[1]
     step = 32
@@ -138,8 +143,10 @@
         stack_kernel,
         grid=(steps,),
         in_specs=[
-            pl.BlockSpec((step, segs, src_count), lambda i: (i, 0, 0)),
-            pl.BlockSpec((step, segs, src_count), lambda i: (i + steps, 0, 0)),
+            pl.BlockSpec((step, segs, end_count), lambda i: (i, 0, 0)),
+            pl.BlockSpec((step, segs, end_count), lambda i: (i + steps, 0, 0)),
+            pl.BlockSpec((step, segs, mid_count), lambda i: (i, 0, 0)),
+            pl.BlockSpec((step, segs, mid_count), lambda i: (i + steps, 0, 0)),
             pl.BlockSpec((step, segs, chans), lambda i: (i, 0, 0)),
             pl.BlockSpec((step, segs, chans), lambda i: (i + steps, 0, 0)),
             whole,
@@ -152,7 +159,7 @@
         cost_estimate=pl.CostEstimate(
             flops=20_000_000_000, bytes_accessed=16_000_000, transcendentals=0
         ),
-    )(sources, sources, channels, channels, high, low)
+    )(ends, ends, middle, middle, channels, channels, high, low)
 
 
 def per_device(raw_strain, gain_index, dead_mask, gain_table, source_index):
@@ -202,17 +209,11 @@
         first_block = spread(offered[cut, :block_src], "fibre", 0)
         last_block = spread(offered[cut, -block_src:], "fibre", fibre_count - 1)
         pieces.append((first_block, last_block))
-    chosen = jnp.concatenate(
-        [
-            jnp.concatenate([piece[0] for piece in pieces], axis=0),
-            middle,
-            jnp.concatenate([piece[1] for piece in pieces], axis=0),
-        ],
-        axis=1,
-    )
+    outer = jnp.concatenate([jnp.concatenate(piece, axis=1) for piece in pieces], axis=0)
 
     whitened = whiten(displacement, table)
-    sources = whiten(chosen, table)
+    ends = jnp.transpose(whiten(outer, table), (2, 0, 1))
+    inner = jnp.transpose(whiten(middle, table), (2, 0, 1))
     channels = jnp.transpose(whitened, (2, 0, 1))
     inverse = lag_table(length, bin_count, bin_count)
     day = lax.axis_index("day")
@@ -221,7 +222,7 @@
     near = [(i, i ^ 1) for i in range(day_count)]
     far = [(i, i ^ 2) for i in range(day_count)]
 
-    lags = stack_lags(jnp.transpose(sources, (2, 0, 1)), channels, inverse)
+    lags = stack_lags(ends, inner, channels, inverse)
     lags = lags.reshape(day_count // 2, 2, part, chan_count, -1)
 
     def pair_sum(value, place, axis, pairs):

time: 286 us -> 329 us (1.15)
  waiting for transfers between devices: 96.4 us -> 147 us
  Pallas kernels: 33.3 us -> 49.5 us
  starting transfers between devices: 50.9 us -> 36.2 us
  other arithmetic: 39.1 us -> 33.3 us
    psum x1, waiting for transfers between devices: 23.9 us -> 79.5 us  [per_device(): middle = lax.psum(offered[:, block_src:-block_src], 'fibre')]
    pallas_call x1, Pallas kernels: 33.3 us -> 49.5 us  [stack_lags(): pl.pallas_call(stack_kernel, grid=(steps,), in_specs=[pl.BlockSpec((step,...]
    ppermute x15, starting transfers between devices: 42.5 us -> 31.1 us  [spread(): block = block + lax.ppermute(block, axis, pairs)]
    reshape x2 -> x3, local copies, waits for them, and re-layouts: 17.7 us -> 22.8 us  [whiten(): return whitened.reshape(segs, rows, length)]
    ppermute x15, waiting for transfers between devices: 44.6 us -> 39.6 us  [spread(): block = block + lax.ppermute(block, axis, pairs)]
    convert_element_type x2 -> x3, other arithmetic: 15.2 us -> 11 us  [whiten(): (spectra * jnp.concatenate([inv_amp, inv_amp], axis=1)).astype(jnp.bfloat16)]
    unnamed x12 -> x6, local copies, waits for them, and re-layouts: 5.71 us -> 1.96 us
    dot_general x2 -> x3, matrix products: 7.3 us -> 6.83 us  [whiten(): jnp.dot(displacement.reshape(-1, length), table, preferred_element_type=j...]
  transfers between devices with their start and end apart: 20 -> 20, of which waited for: 8 -> 9; matrix products, arithmetic and copies ran while one was open for 14% -> 14% of each run, Pallas kernels for 0% -> 0%
where the time goes in v4:
time: 329 us; the launch traced here: 328 us
  waiting for transfers between devices  147 us (45%)
  Pallas kernels  49.5 us (15%)
  starting transfers between devices  36.2 us (11%)
  other arithmetic  33.3 us (10%)
  local copies, waits for them, and re-layouts  28.9 us (9%)
  matrix products  19 us (6%)
  between operations  13.9 us (4%)
    psum x1, waiting for transfers between devices, per_device(): middle = lax.psum(offered[:, block_src:-block_src], 'fibre')  79.5 us
    pallas_call x1, Pallas kernels, stack_lags(): pl.pallas_call(stack_kernel, grid=(steps,), in_specs=[pl.BlockSpec((step,...  49.5 us
    ppermute x15, waiting for transfers between devices, spread(): block = block + lax.ppermute(block, axis, pairs)  39.6 us
    ppermute x15, starting transfers between devices, spread(): block = block + lax.ppermute(block, axis, pairs)  31.1 us
    ppermute x2, waiting for transfers between devices, pair_sum(): came = lax.ppermute(give.astype(jnp.bfloat16), 'day', pairs)  28 us
    reshape x3, local copies, waits for them, and re-layouts, whiten(): return whitened.reshape(segs, rows, length)  22.8 us
    convert_element_type x3, other arithmetic, whiten(): (spectra * jnp.concatenate([inv_amp, inv_amp], axis=1)).astype(jnp.bfloat16)  11 us
    dot_general x3, matrix products, whiten(): jnp.dot(displacement.reshape(-1, length), table, preferred_element_type=j...  6.83 us
  transfers between devices with their start and end apart: 20, of which 9 were waited for; matrix products, arithmetic and copies ran while one was open for 14% of the time, Pallas kernels for 0%

profile of v4, /device:TPU:0, one launch (start us, length us, event | category | flops | bytes accessed | tf_op | source)
XLA Modules:
  0.0 327.8 jit_solution(9486240082602608111)
XLA Ops:
  8.0 5.0 %fusion.1 = bf16[48,128,512]{2,1,0:T(8,128)(2,1)S(1)} fusion(bf16[1,48,128,512]{3,2,1,0:T(8,128)(2,1)} %param.5, f32[128]{0:T(128)S(1)} %convert_multiply_fusion.1), kind=kLoop, calls=%fused_computation.3 | loop fusion | flops 9437184 | bytes 12583424 | tf_op jit(solution)/shard_map/convert_element_type | solution.py:177
  13.4 5.9 %collective-permute-start.2 = (f32[48,512]{1,0:T(8,128)S(1)}, f32[48,512]{1,0:T(8,128)S(1)}, u32[]{:S(2)}, u32[]{:S(2)}) collective-permute-start(f32[48,512]{1,0:T(8,128)S(1)} %broadcast_select_fusion), channel_id=1, source_target_pairs={{0,16},{1,17},{2,18},{3,19}} | collective-permute-start | bytes 294920 | tf_op jit(solution)/shard_map/ppermute | solution.py:79
  19.5 2.2 collective-permute-start
  23.1 2.3 multiply_convert_fusion.1
  26.7 4.5 %collective-permute-start.3 = (f32[48,512]{1,0:T(8,128)S(1)}, f32[48,512]{1,0:T(8,128)S(1)}, u32[]{:S(2)}, u32[]{:S(2)}) collective-permute-start(f32[48,512]{1,0:T(8,128)S(1)} %fusion.97), channel_id=1, source_target_pairs={{0,8},{16,24},{1,9},{17,25},{2,10},{18,26},{3,11},{19,27}} | collective-permute-start | bytes 294920 | tf_op jit(solution)/shard_map/ppermute | solution.py:79
  31.2 2.2 collective-permute-done.3
  34.8 21.8 %collective-permute-done.4 = f32[48,512]{1,0:T(8,128)S(1)} collective-permute-done((f32[48,512]{1,0:T(8,128)S(1)}, f32[48,512]{1,0:T(8,128)S(1)}, u32[]{:S(2)}, u32[]{:S(2)}) %collective-permute-start.4) | collective-permute-done | bytes 98336 | tf_op jit(solution)/shard_map/ppermute | solution.py:79
  56.6 4.5 %multiply_convert_fusion = bf16[48,512,128]{1,2,0:T(8,128)(2,1)S(1)} fusion(f32[48,512]{1,0:T(8,128)S(1)} %add.151, bf16[48,16,512]{2,1,0:T(8,128)(2,1)} %collective-permute-done.1, bf16[48,128,512]{2,1,0:T(8,128)(2,1)} %copy-done.1, bf16[48,16,512]{2,1,0:T(8,128)(2,1)} %collective-permute-done), kind=kOutput, calls=%fused_computation.4 | convolution fusion | flops 1039847424 | bytes 14254080 | tf_op jit(solution)/shard_map/ck,gkt->gct/dot_general | solution.py:190
  62.4 4.3 %collective-permute-start.11 = (bf16[24,16,512]{2,1,0:T(8,128)(2,1)S(1)}, bf16[24,16,512]{2,1,0:T(8,128)(2,1)S(1)}, u32[]{:S(2)}, u32[]{:S(2)}) collective-permute-start(bf16[24,16,512]{2,1,0:T(8,128)(2,1)S(1)} %get-tuple-element.13), channel_id=1, source_target_pairs={{0,16},{1,17},{2,18},{3,19}} | collective-permute-start | bytes 1179656 | tf_op jit(solution)/shard_map/ppermute | solution.py:79
  69.6 3.4 %fusion.59 = f32[6144,512]{1,0:T(8,128)S(1)} fusion(bf16[6144,512]{1,0:T(8,128)(2,1)S(1)} %bitcast.44, bf16[512,256]{1,0:T(8,128)(2,1)S(1)} %get-tuple-element.19, bf16[512,256]{1,0:T(8,128)(2,1)S(1)} %get-tuple-element.20), kind=kOutput, calls=%fused_computation.88 | convolution fusion | flops 3222274048 | bytes 19398656 | tf_op jit(solution)/shard_map/dot_general | solution.py:63
  74.1 2.1 collective-permute-done.11
  76.2 7.3 %collective-permute-done.5 = bf16[24,16,512]{2,1,0:T(8,128)(2,1)S(1)} collective-permute-done((bf16[24,16,512]{2,1,0:T(8,128)(2,1)S(1)}, bf16[24,16,512]{2,1,0:T(8,128)(2,1)S(1)}, u32[]{:S(2)}, u32[]{:S(2)}) %collective-permute-start.5) | collective-permute-done | bytes 393248 | tf_op jit(solution)/shard_map/ppermute | solution.py:79
  87.7 3.7 %fusion.10 = f32[6144,256]{1,0:T(8,128)} fusion(f32[6144,256]{1,0:T(8,128)S(1)} %fusion.31, f32[256]{0:T(256)S(1)} %convert_reduce_fusion, f32[6144,512]{1,0:T(8,128)S(1)} %fusion.59), kind=kOutput, calls=%fused_computation.14 | convolution fusion | flops 821231616 | bytes 25166848 | tf_op jit(solution)/shard_map/dot_general | solution.py:44
  91.4 3.1 collective-permute-done.6
  94.7 2.0 collective-permute-start.7
  98.1 3.0 collective-permute-done.12
  101.3 3.4 %collective-permute-start.13 = (bf16[24,16,512]{2,1,0:T(8,128)(2,1)S(1)}, bf16[24,16,512]{2,1,0:T(8,128)(2,1)}, u32[]{:S(2)}, u32[]{:S(2)}) collective-permute-start(bf16[24,16,512]{2,1,0:T(8,128)(2,1)S(1)} %add.161), channel_id=1, source_target_pairs={{0,4},{8,12},{16,20},{24,28},{1,5},{9,13},{17,21},{25,29},{2,6},{1... | collective-permute-start | bytes 1179656 | tf_op jit(solution)/shard_map/ppermute | solution.py:79
  105.6 1.5 collective-permute-start.16
  107.1 9.6 %fusion = bf16[6144,512]{1,0:T(8,128)(2,1)} fusion(f32[6144,512]{1,0:T(8,128)S(1)} %fusion.59, f32[6144,256]{1,0:T(8,128)} %fusion.10), kind=kLoop, calls=%fused_computation.1 | loop fusion | flops 9437184 | bytes 25165824 | tf_op jit(solution)/shard_map/convert_element_type | solution.py:70
  118.0 9.1 %copy.42 = bf16[48,128,512]{1,0,2:T(8,128)(2,1)} copy(bf16[48,128,512]{2,1,0:T(8,128)(2,1)} %bitcast.45) | data formatting | bytes 12582912 | tf_op jit(solution)/shard_map/reshape | solution.py:71
  133.5 6.8 %copy.28 = bf16[48,32,512]{1,0,2:T(8,128)(2,1)} copy(bf16[48,32,512]{2,1,0:T(8,128)(2,1)S(1)} %bitcast.54) | data formatting | bytes 3145728 | tf_op jit(solution)/shard_map/reshape | solution.py:71
  140.3 79.5 %all-reduce.2.cloned.1.call-done = bf16[1536,512]{1,0:T(8,128)(2,1)} async-done(((bf16[1536,512]{1,0:T(8,128)(2,1)}), bf16[1536,512]{1,0:T(8,128)(2,1)}) %all-reduce.2.cloned.1.call-update) | async-done | bytes 1572880 | tf_op jit(solution)/shard_map/psum | solution.py:204
  219.8 2.4 fusion.60
  223.8 6.9 %copy.31 = bf16[48,32,512]{1,0,2:T(8,128)(2,1)} copy(bf16[48,32,512]{2,1,0:T(8,128)(2,1)S(1)} %bitcast.55) | data formatting | bytes 3145728 | tf_op jit(solution)/shard_map/reshape | solution.py:71
  230.7 49.5 %shard_map.55 = f32[64,128,256]{2,1,0:T(8,128)} custom-call(bf16[512,48,32]{2,1,0:T(8,128)(2,1)} %bitcast.50, bf16[512,48,32]{2,1,0:T(8,128)(2,1)} %bitcast.51, bf16[512,48,32]{2,1,0:T(8,128)(2,1)} %bitcast.52, bf16[512,48,32]{2,1,0:T(8,128)(2,1)} %bitcast.53, bf16[512,48,128]{2,1,0:T(8,128)(2,1)} %bitcast.47, bf16[512,48,128]{2,1,0:T(8,128)(2,1)} %bitcast.48, ...), custom_call_target="tpu_custom_call" | custom-call | flops 20000000000 | bytes 16000000 | tf_op jit(solution)/shard_map/pallas_call | solution.py:142
  280.2 2.5 fusion.26
  282.8 4.2 %collective-permute-done.17 = bf16[2,16,128,256]{3,2,1,0:T(8,128)(2,1)} collective-permute-done((bf16[2,16,128,256]{3,2,1,0:T(8,128)(2,1)S(1)}, bf16[2,16,128,256]{3,2,1,0:T(8,128)(2,1)}, u32[]{:S(2)}, u32[]{:S(2)}) %collective-permute-start.17) | collective-permute-done | bytes 2097184 | tf_op jit(solution)/shard_map/ppermute | solution.py:231
  287.0 3.4 %bitcast_add_fusion = f32[2,16,128,256]{3,2,1,0:T(8,128)S(1)} fusion(bf16[2,16,128,256]{3,2,1,0:T(8,128)(2,1)} %collective-permute-done.17, f32[2,2,16,128,256]{4,3,2,1,0:T(8,128)} %bitcast.57, s32[]{:T(128)S(6)} %select_n.97), kind=kLoop, calls=%fused_computation.22 | loop fusion | flops 2097152 | bytes 10485764 | tf_op jit(solution)/shard_map/add | solution.py:232
  290.4 1.9 copy-done
  292.5 1.5 collective-permute-start.18
  294.0 23.7 %collective-permute-done.18 = bf16[16,128,256]{2,1,0:T(8,128)(2,1)S(1)} collective-permute-done((bf16[16,128,256]{2,1,0:T(8,128)(2,1)S(1)}, bf16[16,128,256]{2,1,0:T(8,128)(2,1)S(1)}, u32[]{:S(2)}, u32[]{:S(2)}) %collective-permute-start.18) | collective-permute-done | bytes 1048608 | tf_op jit(solution)/shard_map/ppermute | solution.py:231
  317.8 3.2 fusion.27
  (70 shorter events, 27.4 us)
Async XLA Ops:
  6.5 213.2 %all-reduce.2.cloned.1.call-start = ((), (), s32[]{:S(2)}) async-start(), calls=%async_computation | async-start | bytes 3145728 | tf_op jit(solution)/shard_map/psum | solution.py:204
  13.0 6.4 %copy-start.1 = (bf16[48,128,512]{2,1,0:T(8,128)(2,1)}, bf16[48,128,512]{2,1,0:T(8,128)(2,1)S(1)}, u32[]{:S(2)}) copy-start(bf16[48,128,512]{2,1,0:T(8,128)(2,1)S(1)} %fusion.1) | copy-start | bytes 18874372
  13.0 13.5 %copy-start.2 = (s32[4,16]{1,0:T(4,128)S(1)}, s32[4,16]{1,0:T(4,128)}, u32[]{:S(2)}) copy-start(s32[4,16]{1,0:T(4,128)} %param.9) | copy-start | bytes 772
  13.4 13.3 %collective-permute-start.2 = (f32[48,512]{1,0:T(8,128)S(1)}, f32[48,512]{1,0:T(8,128)S(1)}, u32[]{:S(2)}, u32[]{:S(2)}) collective-permute-start(f32[48,512]{1,0:T(8,128)S(1)} %broadcast_select_fusion), channel_id=1, source_target_pairs={{0,16},{1,17},{2,18},{3,19}} | collective-permute-start | bytes 294920 | tf_op jit(solution)/shard_map/ppermute | solution.py:79
  19.5 37.1 %collective-permute-start = (bf16[48,16,512]{2,1,0:T(8,128)(2,1)S(1)}, bf16[48,16,512]{2,1,0:T(8,128)(2,1)}, u32[]{:S(2)}, u32[]{:S(2)}) collective-permute-start(bf16[48,16,512]{2,1,0:T(8,128)(2,1)S(1)} %get-tuple-element.5), channel_id=1, source_target_pairs={{0,4},{4,8},{8,12},{12,16},{16,20},{20,24},{24,28},{1,5},{5,9},{9,... | collective-permute-start | bytes 2359304 | tf_op jit(solution)/shard_map/ppermute | solution.py:17
  21.7 34.9 %collective-permute-start.1 = (bf16[48,16,512]{2,1,0:T(8,128)(2,1)S(1)}, bf16[48,16,512]{2,1,0:T(8,128)(2,1)}, u32[]{:S(2)}, u32[]{:S(2)}) collective-permute-start(bf16[48,16,512]{2,1,0:T(8,128)(2,1)S(1)} %get-tuple-element.6), channel_id=1, source_target_pairs={{4,0},{8,4},{12,8},{16,12},{20,16},{24,20},{28,24},{5,1},{9,5},{13... | collective-permute-start | bytes 2359304 | tf_op jit(solution)/shard_map/ppermute | solution.py:18
  26.7 6.7 %collective-permute-start.3 = (f32[48,512]{1,0:T(8,128)S(1)}, f32[48,512]{1,0:T(8,128)S(1)}, u32[]{:S(2)}, u32[]{:S(2)}) collective-permute-start(f32[48,512]{1,0:T(8,128)S(1)} %fusion.97), channel_id=1, source_target_pairs={{0,8},{16,24},{1,9},{17,25},{2,10},{18,26},{3,11},{19,27}} | collective-permute-start | bytes 294920 | tf_op jit(solution)/shard_map/ppermute | solution.py:79
  33.4 23.2 %collective-permute-start.4 = (f32[48,512]{1,0:T(8,128)S(1)}, f32[48,512]{1,0:T(8,128)S(1)}, u32[]{:S(2)}, u32[]{:S(2)}) collective-permute-start(f32[48,512]{1,0:T(8,128)S(1)} %add.150), channel_id=1, source_target_pairs={{0,4},{8,12},{16,20},{24,28},{1,5},{9,13},{17,21},{25,29},{2,6},{1... | collective-permute-start | bytes 294920 | tf_op jit(solution)/shard_map/ppermute | solution.py:79
  62.4 13.8 %collective-permute-start.11 = (bf16[24,16,512]{2,1,0:T(8,128)(2,1)S(1)}, bf16[24,16,512]{2,1,0:T(8,128)(2,1)S(1)}, u32[]{:S(2)}, u32[]{:S(2)}) collective-permute-start(bf16[24,16,512]{2,1,0:T(8,128)(2,1)S(1)} %get-tuple-element.13), channel_id=1, source_target_pairs={{0,16},{1,17},{2,18},{3,19}} | collective-permute-start | bytes 1179656 | tf_op jit(solution)/shard_map/ppermute | solution.py:79
  66.7 9.5 %collective-permute-start.14 = (bf16[24,16,512]{2,1,0:T(8,128)(2,1)S(1)}, bf16[24,16,512]{2,1,0:T(8,128)(2,1)S(1)}, u32[]{:S(2)}, u32[]{:S(2)}) collective-permute-start(bf16[24,16,512]{2,1,0:T(8,128)(2,1)S(1)} %get-tuple-element.12), channel_id=1, source_target_pairs={{28,12},{29,13},{30,14},{31,15}} | collective-permute-start | bytes 1179656 | tf_op jit(solution)/shard_map/ppermute | solution.py:79
  67.4 16.1 %collective-permute-start.5 = (bf16[24,16,512]{2,1,0:T(8,128)(2,1)S(1)}, bf16[24,16,512]{2,1,0:T(8,128)(2,1)S(1)}, u32[]{:S(2)}, u32[]{:S(2)}) collective-permute-start(bf16[24,16,512]{2,1,0:T(8,128)(2,1)S(1)} %get-tuple-element.11), channel_id=1, source_target_pairs={{0,16},{1,17},{2,18},{3,19}} | collective-permute-start | bytes 1179656 | tf_op jit(solution)/shard_map/ppermute | solution.py:79
  68.7 14.8 %collective-permute-start.8 = (bf16[24,16,512]{2,1,0:T(8,128)(2,1)S(1)}, bf16[24,16,512]{2,1,0:T(8,128)(2,1)S(1)}, u32[]{:S(2)}, u32[]{:S(2)}) collective-permute-start(bf16[24,16,512]{2,1,0:T(8,128)(2,1)S(1)} %get-tuple-element.14), channel_id=1, source_target_pairs={{28,12},{29,13},{30,14},{31,15}} | collective-permute-start | bytes 1179656 | tf_op jit(solution)/shard_map/ppermute | solution.py:79
  83.7 10.9 %collective-permute-start.6 = (bf16[24,16,512]{2,1,0:T(8,128)(2,1)S(1)}, bf16[24,16,512]{2,1,0:T(8,128)(2,1)S(1)}, u32[]{:S(2)}, u32[]{:S(2)}) collective-permute-start(bf16[24,16,512]{2,1,0:T(8,128)(2,1)S(1)} %get-tuple-element.7), channel_id=1, source_target_pairs={{0,8},{16,24},{1,9},{17,25},{2,10},{18,26},{3,11},{19,27}} | collective-permute-start | bytes 1179656 | tf_op jit(solution)/shard_map/ppermute | solution.py:79
  85.0 11.7 %collective-permute-start.9 = (bf16[24,16,512]{2,1,0:T(8,128)(2,1)S(1)}, bf16[24,16,512]{2,1,0:T(8,128)(2,1)S(1)}, u32[]{:S(2)}, u32[]{:S(2)}) collective-permute-start(bf16[24,16,512]{2,1,0:T(8,128)(2,1)S(1)} %get-tuple-element.8), channel_id=1, source_target_pairs={{28,20},{12,4},{29,21},{13,5},{30,22},{14,6},{31,23},{15,7}} | collective-permute-start | bytes 1179656 | tf_op jit(solution)/shard_map/ppermute | solution.py:79
  85.7 15.5 %collective-permute-start.12 = (bf16[24,16,512]{2,1,0:T(8,128)(2,1)S(1)}, bf16[24,16,512]{2,1,0:T(8,128)(2,1)S(1)}, u32[]{:S(2)}, u32[]{:S(2)}) collective-permute-start(bf16[24,16,512]{2,1,0:T(8,128)(2,1)S(1)} %get-tuple-element.9), channel_id=1, source_target_pairs={{0,8},{16,24},{1,9},{17,25},{2,10},{18,26},{3,11},{19,27}} | collective-permute-start | bytes 1179656 | tf_op jit(solution)/shard_map/ppermute | solution.py:79
  87.0 17.7 %collective-permute-start.15 = (bf16[24,16,512]{2,1,0:T(8,128)(2,1)S(1)}, bf16[24,16,512]{2,1,0:T(8,128)(2,1)S(1)}, u32[]{:S(2)}, u32[]{:S(2)}) collective-permute-start(bf16[24,16,512]{2,1,0:T(8,128)(2,1)S(1)} %get-tuple-element.10), channel_id=1, source_target_pairs={{28,20},{12,4},{29,21},{13,5},{30,22},{14,6},{31,23},{15,7}} | collective-permute-start | bytes 1179656 | tf_op jit(solution)/shard_map/ppermute | solution.py:79
  94.7 32.4 %collective-permute-start.7 = (bf16[24,16,512]{2,1,0:T(8,128)(2,1)S(1)}, bf16[24,16,512]{2,1,0:T(8,128)(2,1)}, u32[]{:S(2)}, u32[]{:S(2)}) collective-permute-start(bf16[24,16,512]{2,1,0:T(8,128)(2,1)S(1)} %add.155), channel_id=1, source_target_pairs={{0,4},{8,12},{16,20},{24,28},{1,5},{9,13},{17,21},{25,29},{2,6},{1... | collective-permute-start | bytes 1179656 | tf_op jit(solution)/shard_map/ppermute | solution.py:79
  96.8 31.4 %collective-permute-start.10 = (bf16[24,16,512]{2,1,0:T(8,128)(2,1)S(1)}, bf16[24,16,512]{2,1,0:T(8,128)(2,1)S(1)}, u32[]{:S(2)}, u32[]{:S(2)}) collective-permute-start(bf16[24,16,512]{2,1,0:T(8,128)(2,1)S(1)} %add.158), channel_id=1, source_target_pairs={{28,24},{20,16},{12,8},{4,0},{29,25},{21,17},{13,9},{5,1},{30,26},... | collective-permute-start | bytes 1179656 | tf_op jit(solution)/shard_map/ppermute | solution.py:79
  101.3 27.0 %collective-permute-start.13 = (bf16[24,16,512]{2,1,0:T(8,128)(2,1)S(1)}, bf16[24,16,512]{2,1,0:T(8,128)(2,1)}, u32[]{:S(2)}, u32[]{:S(2)}) collective-permute-start(bf16[24,16,512]{2,1,0:T(8,128)(2,1)S(1)} %add.161), channel_id=1, source_target_pairs={{0,4},{8,12},{16,20},{24,28},{1,5},{9,13},{17,21},{25,29},{2,6},{1... | collective-permute-start | bytes 1179656 | tf_op jit(solution)/shard_map/ppermute | solution.py:79
  105.6 23.9 %collective-permute-start.16 = (bf16[24,16,512]{2,1,0:T(8,128)(2,1)}, bf16[24,16,512]{2,1,0:T(8,128)(2,1)}, u32[]{:S(2)}, u32[]{:S(2)}) collective-permute-start(bf16[24,16,512]{2,1,0:T(8,128)(2,1)} %add.164), channel_id=1, source_target_pairs={{28,24},{20,16},{12,8},{4,0},{29,25},{21,17},{13,9},{5,1},{30,26},... | collective-permute-start | bytes 1179656 | tf_op jit(solution)/shard_map/ppermute | solution.py:79
  282.6 4.4 %collective-permute-start.17 = (bf16[2,16,128,256]{3,2,1,0:T(8,128)(2,1)S(1)}, bf16[2,16,128,256]{3,2,1,0:T(8,128)(2,1)}, u32[]{:S(2)}, u32[]{:S(2)}) collective-permute-start(bf16[2,16,128,256]{3,2,1,0:T(8,128)(2,1)S(1)} %fusion.26), channel_id=1, source_target_pairs={{0,1},{1,0},{2,3},{3,2},{4,5},{5,4},{6,7},{7,6},{8,9},{9,8},{10,11... | collective-permute-start | bytes 6291464 | tf_op jit(solution)/shard_map/ppermute | solution.py:231
  290.4 2.0 copy-start
  292.5 25.3 %collective-permute-start.18 = (bf16[16,128,256]{2,1,0:T(8,128)(2,1)S(1)}, bf16[16,128,256]{2,1,0:T(8,128)(2,1)S(1)}, u32[]{:S(2)}, u32[]{:S(2)}) collective-permute-start(bf16[16,128,256]{2,1,0:T(8,128)(2,1)S(1)} %fusion.35), channel_id=1, source_target_pairs={{0,2},{1,3},{2,0},{3,1},{4,6},{5,7},{6,4},{7,5},{8,10},{9,11},{10,... | collective-permute-start | bytes 3145736 | tf_op jit(solution)/shard_map/ppermute | solution.py:231
Sparse Core Ops, SparseCore 0:
  127.2 92.5 all-reduce.1
